TPU v7x, 32 devices: a whole 2x2x4 slice. The times are simulated.
32 devices in a mesh: dp: 8 (over y, x, core), seq: 4 (over z).
Axes of the slice: x: 2, y: 2, z: 4, core: 2. Of those that a mesh axis runs over, the one named last changes fastest.
Arguments:
- token_rows: bfloat16 [40960, 5120], P(('dp', 'seq')), may hold values from -6 to 6
- key_rows: bfloat16 [40960, 128], P(('dp', 'seq')), may hold values from -1.8 to 1.8
- query_rows: bfloat16 [40960, 128], P(('dp', 'seq')), may hold values from -0.1796875 to 0.1796875
- step_rows: bfloat16 [40960, 80], P(('dp', 'seq')), may hold values from -6 to 1000
- decay_log: float32 [80], replicated, may hold values from -9.3 to -1.8
- skip_gain: float32 [80], replicated, may hold values from 0.5 to 1.5
- source_rows: int32 [8, 5120], P('dp', 'seq'), may hold values from 0 to 40959, as said below
- document_starts: int32 [8, 6], P('dp'), may hold values from 0 to 5119, as said below
Outputs:
- layer_result_rows: bfloat16 [8, 5120, 5120], P('dp', 'seq')
Inputs may be any that keep to these rules, and one draw needn't show every extreme that they name: `source_rows`: every loaded row is placed exactly once. The row at position p of a packed sequence is held by a device whose seq index is p // 1280. Positions come in aligned runs of 8 that hold consecutive rows of one device. A device takes at most 168 of its positions from any one device, and in every seq index some pair of devices reaches that number. `document_starts`: each row is strictly increasing and begins with 0.
All inputs are finite; a program needn't handle non-finite values.
Results may differ from a plain program's by a relative error of at most 0.0065.
Values may be sent and summed in bfloat16 or wider, within the bound.
A program may use at most 192 MiB of HBM per device.

v0:
```python
import functools

import jax
import jax.numpy as jnp
from jax import lax
from jax.experimental import pallas as pl
from jax.experimental.pallas import tpu as pltpu
from jax.sharding import PartitionSpec as P

SPAN = 256
SEG = 8
RUNS = SPAN // SEG
HALF = SPAN // 2
LANES = 128
CHUNK_HEADS = 16

f32, bf16 = jnp.float32, jnp.bfloat16
ANY = pl.BlockSpec(memory_space=pl.ANY)
VMEM_LIMIT = 60 * 1024 * 1024


def params(**more):
    return pltpu.CompilerParams(vmem_limit_bytes=VMEM_LIMIT, **more)


def whole(shape):
    return pl.BlockSpec(shape, lambda *_: (0,) * len(shape))


def spread(hilo, ones):
    return jnp.dot(hilo, ones, preferred_element_type=f32)


def split_float(value):
    high = value.astype(bf16)
    low = (value - high.astype(f32)).astype(bf16)
    return jnp.concatenate([high, low], axis=1)


def plan_kernel(groups, shards, runs, capacity, me_ref, wanted_ref, own_ref, send_ref, pick_ref):
    me = me_ref[0]
    earlier = lax.broadcasted_iota(jnp.int32, (runs, runs), 0) < lax.broadcasted_iota(
        jnp.int32, (runs, runs), 1
    )
    earlier = jnp.where(earlier, 1.0, 0.0).astype(bf16)

    def ranks(hit):
        ones = jnp.where(hit, 1.0, 0.0).astype(bf16)
        return jnp.dot(ones, earlier, preferred_element_type=f32).astype(jnp.int32)

    wanted = wanted_ref[...]
    mine = (wanted // runs) // shards == me
    local = wanted % runs
    rank = ranks(mine)
    lane = lax.broadcasted_iota(jnp.int32, (groups, LANES), 1)
    send = jnp.zeros((groups, LANES), jnp.int32)
    for slot in range(capacity):
        chosen = jnp.sum(jnp.where(mine & (rank == slot), local, 0), axis=1, keepdims=True)
        send = jnp.where(lane == slot, chosen, send)
    send_ref[...] = send
    source = (own_ref[...] // runs) // shards
    group = lax.broadcasted_iota(jnp.int32, (groups, runs), 0)
    hit = jnp.broadcast_to(source, (groups, runs)) == group
    pick_ref[...] = jnp.sum(
        jnp.where(hit, group * capacity + ranks(hit), 0), axis=0, keepdims=True
    )


def make_plan(groups, shards, runs, capacity, me, wanted, own):
    send, pick = pl.pallas_call(
        functools.partial(plan_kernel, groups, shards, runs, capacity),
        grid_spec=pltpu.PrefetchScalarGridSpec(
            num_scalar_prefetch=1,
            grid=(1,),
            in_specs=[whole((groups, runs)), whole((1, runs))],
            out_specs=[whole((groups, LANES)), whole((1, runs))],
        ),
        out_shape=[
            jax.ShapeDtypeStruct((groups, LANES), jnp.int32),
            jax.ShapeDtypeStruct((1, runs), jnp.int32),
        ],
        compiler_params=params(),
        name="plan",
    )(me, wanted, own)
    return send, pick[0]


def collect_kernel(groups, capacity, column, width, send_ref, rows_ref, token_ref, out_ref, held, gets, puts):
    def put(group):
        return pltpu.make_async_copy(held.at[group], out_ref.at[group], puts.at[group])

    for group in range(groups):

        @pl.loop(0, capacity)
        def _(slot):
            pltpu.make_async_copy(
                rows_ref.at[send_ref[group, slot], :, pl.ds(column, width)],
                held.at[group, slot],
                gets.at[group],
            ).start()

    for group in range(groups):
        pltpu.make_async_copy(held.at[group], held.at[group], gets.at[group]).wait()
        put(group).start()
    for group in range(groups):
        put(group).wait()


def collect(send, rows, token, groups, capacity, column, width):
    return pl.pallas_call(
        functools.partial(collect_kernel, groups, capacity, column, width),
        grid_spec=pltpu.PrefetchScalarGridSpec(
            num_scalar_prefetch=1,
            grid=(1,),
            in_specs=[ANY, ANY],
            out_specs=ANY,
            scratch_shapes=[
                pltpu.VMEM((groups, capacity, SEG, width), bf16),
                pltpu.SemaphoreType.DMA((groups,)),
                pltpu.SemaphoreType.DMA((groups,)),
            ],
        ),
        out_shape=jax.ShapeDtypeStruct((groups, capacity, SEG, width), bf16),
        compiler_params=params(),
        cost_estimate=pl.CostEstimate(
            flops=0, transcendentals=0, bytes_accessed=4 * groups * capacity * SEG * width
        ),
        name="collect",
    )(send, rows, token)


def fetch_spans(spans, pick_ref, source_ref, held, sems):
    @pl.when(pl.program_id(0) == 0)
    def _():
        @pl.loop(0, spans * RUNS)
        def _(run):
            pltpu.make_async_copy(
                source_ref.at[pick_ref[run]], held.at[run], sems.at[run // RUNS]
            ).start()


def fetched(held, sems, span):
    part = held.at[pl.ds(span * RUNS, RUNS)]
    pltpu.make_async_copy(part, part, sems.at[span]).wait()
    value = held[pl.ds(span * RUNS, RUNS)].astype(f32)
    return value.reshape(SPAN, value.shape[-1])


def prepare_kernel(
    spans, starts_count, pick_ref, starts_ref, small_ref, decay_ref,
    cum_ref, bias_ref, entry_ref, end_ref, device_ref, through_ref, keys_ref, query_ref, score_ref,
    held, sems, later,
):
    step = pl.program_id(0)
    span = spans - 1 - step

    @pl.when(step == 0)
    def _():
        @pl.loop(0, spans * RUNS)
        def _(run):
            pltpu.make_async_copy(
                small_ref.at[pick_ref[run]], held.at[run], sems.at[run // RUNS]
            ).start()

        later[...] = jnp.zeros_like(later)

    small = fetched(held, sems, span)
    keys = small[:, :LANES]
    query = small[:, LANES : 2 * LANES]
    raw = small[:, 2 * LANES :]
    steps = jnp.maximum(raw, 0.0) + jnp.log1p(jnp.exp(-jnp.abs(raw)))
    rate = jnp.exp(decay_ref[...])
    log_decay = -steps * rate
    row = lax.broadcasted_iota(jnp.int32, (SPAN, SPAN), 0)
    col = lax.broadcasted_iota(jnp.int32, (SPAN, SPAN), 1)
    lower = jnp.where(col <= row, 1.0, 0.0)
    cum = jnp.dot(lower, log_decay, precision=lax.Precision.HIGHEST, preferred_element_type=f32)
    low = span * SPAN
    doc_row = jnp.zeros((SPAN, SPAN), jnp.int32)
    doc_col = jnp.zeros((SPAN, SPAN), jnp.int32)
    doc = jnp.zeros((SPAN, LANES), jnp.int32)
    last = jnp.int32(0)
    after = jnp.int32(0)
    row_lanes = row[:, :LANES]
    for number in range(starts_count):
        start = starts_ref[number] - low
        inside = (start >= 0) & (start < SPAN)
        at = jnp.where(inside, start, jnp.int32(1 << 20))
        doc_row += (row >= at).astype(jnp.int32)
        doc_col += (col >= at).astype(jnp.int32)
        doc += (row_lanes >= at).astype(jnp.int32)
        last += inside.astype(jnp.int32)
        after += ((start >= SPAN) & (start < (spans - span) * SPAN)).astype(jnp.int32)
    linked = (doc_row == doc_col) & (col <= row)
    scores = lax.dot_general(
        query.astype(bf16), keys.astype(bf16), (((1,), (1,)), ((), ())), preferred_element_type=f32
    )
    score_ref[0] = jnp.where(linked, scores, 0.0)
    total = cum[SPAN - 1 :, :]
    to_end = total - cum
    entry_ref[...] = split_float(jnp.where(doc == 0, jnp.exp(cum), 0.0))
    at_end = doc == last
    end_ref[...] = split_float(jnp.where(at_end, jnp.exp(to_end), 0.0) * steps)
    reach = at_end & (after == 0)
    device_ref[...] = split_float(jnp.where(reach, jnp.exp(to_end + later[...]), 0.0) * steps)
    cum_ref[...] = cum
    bias_ref[...] = (jnp.log(steps) - cum).T
    keys_ref[...] = keys.T.astype(bf16)
    query_ref[...] = query.astype(bf16)
    later[...] = later[...] + total
    through_ref[...] = jnp.where(last + after == 0, jnp.exp(later[...]), 0.0)


def prepare(pick, starts, small, decay, tokens):
    spans = tokens // SPAN
    starts_count = starts.shape[0]

    def back(step, *_):
        return (spans - 1 - step, 0)

    def back_lanes(step, *_):
        return (0, spans - 1 - step)

    def rows(width):
        return pl.BlockSpec((SPAN, width), back)

    return pl.pallas_call(
        functools.partial(prepare_kernel, spans, starts_count),
        grid_spec=pltpu.PrefetchScalarGridSpec(
            num_scalar_prefetch=2,
            grid=(spans,),
            in_specs=[ANY, whole((1, LANES))],
            out_specs=[
                rows(LANES),
                pl.BlockSpec((LANES, SPAN), back_lanes),
                rows(2 * LANES),
                rows(2 * LANES),
                rows(2 * LANES),
                whole((1, LANES)),
                pl.BlockSpec((LANES, SPAN), back_lanes),
                rows(LANES),
                pl.BlockSpec((1, SPAN, SPAN), lambda step, *_: (spans - 1 - step, 0, 0)),
            ],
            scratch_shapes=[
                pltpu.VMEM((tokens // SEG, SEG, 3 * LANES), bf16),
                pltpu.SemaphoreType.DMA((spans,)),
                pltpu.VMEM((1, LANES), f32),
            ],
        ),
        out_shape=[
            jax.ShapeDtypeStruct((tokens, LANES), f32),
            jax.ShapeDtypeStruct((LANES, tokens), f32),
            jax.ShapeDtypeStruct((tokens, 2 * LANES), bf16),
            jax.ShapeDtypeStruct((tokens, 2 * LANES), bf16),
            jax.ShapeDtypeStruct((tokens, 2 * LANES), bf16),
            jax.ShapeDtypeStruct((1, LANES), f32),
            jax.ShapeDtypeStruct((LANES, tokens), bf16),
            jax.ShapeDtypeStruct((tokens, LANES), bf16),
            jax.ShapeDtypeStruct((spans, SPAN, SPAN), f32),
        ],
        compiler_params=params(),
        name="prepare",
    )(pick, starts, small, decay)


def state_kernel(spans, pick_ref, values_ref, keys_ref, device_ref, ones_ref, out_ref, held, sems):
    span = pl.program_id(0)
    fetch_spans(spans, pick_ref, values_ref, held, sems)

    @pl.when(span == 0)
    def _():
        out_ref[...] = jnp.zeros_like(out_ref)

    values = fetched(held, sems, span)
    scaled = (values * spread(device_ref[...], ones_ref[...])).astype(bf16)
    out_ref[...] += jnp.dot(keys_ref[...], scaled, preferred_element_type=f32)


def final_state(pick, values, keys, device, ones, tokens):
    spans = tokens // SPAN
    width = values.shape[-1]
    return pl.pallas_call(
        functools.partial(state_kernel, spans),
        grid_spec=pltpu.PrefetchScalarGridSpec(
            num_scalar_prefetch=1,
            grid=(spans,),
            in_specs=[
                ANY,
                pl.BlockSpec((LANES, SPAN), lambda s, *_: (0, s)),
                pl.BlockSpec((SPAN, 2 * LANES), lambda s, *_: (s, 0)),
                whole((2 * LANES, width)),
            ],
            out_specs=whole((LANES, width)),
            scratch_shapes=[
                pltpu.VMEM((tokens // SEG, SEG, width), bf16),
                pltpu.SemaphoreType.DMA((spans,)),
            ],
        ),
        out_shape=jax.ShapeDtypeStruct((LANES, width), f32),
        compiler_params=params(),
        cost_estimate=pl.CostEstimate(
            flops=6 * tokens * LANES * width, transcendentals=0, bytes_accessed=2 * tokens * width
        ),
        name="final_state",
    )(pick, values, keys, device, ones)


def layer_kernel(
    spans, first_head, heads, head_width, aliased, pick_ref, values_ref, cum_ref, bias_ref, entry_ref,
    end_ref, keys_ref, query_ref, score_ref, ones_ref, skip_ref, incoming_ref, *rest
):
    out_ref, held, sems, state, base = rest[1:] if aliased else rest
    span = pl.program_id(0)
    fetch_spans(spans, pick_ref, values_ref, held, sems)

    @pl.when(span == 0)
    def _():
        state[...] = incoming_ref[...]

    values = fetched(held, sems, span)
    ones = ones_ref[...]
    entry = spread(entry_ref[...], ones)
    from_state = jnp.dot(query_ref[...], state[...].astype(bf16), preferred_element_type=f32)
    base[...] = from_state * entry + skip_ref[...] * values
    scaled = (values * spread(end_ref[...], ones)).astype(bf16)
    added = jnp.dot(keys_ref[...], scaled, preferred_element_type=f32)
    state[...] = entry[SPAN - 1 :, :] * state[...] + added
    packed = values.astype(bf16)
    per_tile = LANES // head_width
    lane = lax.broadcasted_iota(jnp.int32, (HALF, LANES), 1) // head_width
    for tile in range(heads // per_tile):
        columns = slice(tile * LANES, (tile + 1) * LANES)
        for half in range(2):
            rows = slice(half * HALF, (half + 1) * HALF)
            depth = (half + 1) * HALF
            scores = score_ref[0, rows, :depth]
            total = None
            for inner in range(per_tile):
                head = first_head + tile * per_tile + inner
                gap = cum_ref[rows, head : head + 1] + bias_ref[head : head + 1, :depth]
                weights = (scores * jnp.exp(jnp.minimum(gap, 60.0))).astype(bf16)
                part = jnp.dot(weights, packed[:depth, columns], preferred_element_type=f32)
                total = part if total is None else jnp.where(lane == inner, part, total)
            out_ref[rows, columns] = (base[rows, columns] + total).astype(bf16)


def layer(result, pick, values, prepared, ones, skip, incoming, tokens, full, column, first_head, heads):
    cum, bias, entry, end, keys, query, scores = prepared
    spans = tokens // SPAN
    width = values.shape[-1]
    aliased = result is not None

    def rows(lanes):
        return pl.BlockSpec((SPAN, lanes), lambda s, *_: (s, 0))

    def lanes():
        return pl.BlockSpec((LANES, SPAN), lambda s, *_: (0, s))

    operands = [pick, values, cum, bias, entry, end, keys, query, scores, ones, skip, incoming]
    in_specs = [
        ANY, rows(LANES), lanes(), rows(2 * LANES), rows(2 * LANES), lanes(), rows(LANES),
        pl.BlockSpec((1, SPAN, SPAN), lambda s, *_: (s, 0, 0)),
        whole((2 * LANES, width)), whole((1, width)), whole((LANES, width)),
    ]
    if aliased:
        operands.append(result)
        in_specs.append(ANY)
    return pl.pallas_call(
        functools.partial(
            layer_kernel, spans, first_head, heads, width // heads, aliased
        ),
        grid_spec=pltpu.PrefetchScalarGridSpec(
            num_scalar_prefetch=1,
            grid=(spans,),
            in_specs=in_specs,
            out_specs=pl.BlockSpec((SPAN, width), lambda s, *_: (s, column // width)),
            scratch_shapes=[
                pltpu.VMEM((tokens // SEG, SEG, width), bf16),
                pltpu.SemaphoreType.DMA((spans,)),
                pltpu.VMEM((LANES, width), f32),
                pltpu.VMEM((SPAN, width), f32),
            ],
        ),
        out_shape=jax.ShapeDtypeStruct((tokens, full), bf16),
        input_output_aliases={len(operands) - 1: 0} if aliased else {},
        compiler_params=params(),
        cost_estimate=pl.CostEstimate(
            flops=8 * tokens * SPAN * width, transcendentals=tokens * SPAN * heads,
            bytes_accessed=4 * tokens * width,
        ),
        name="layer",
    )(*operands)


def shifted(block, axis, distance):
    devices = range(lax.axis_size(axis))
    route = [(i - distance, i) for i in devices if i - distance in devices]
    return lax.ppermute(block, axis, route)


def on_device(
    token_rows, key_rows, query_rows, step_rows, decay_log, skip_gain, source_rows, document_starts
):
    tokens, full = token_rows.shape
    groups = lax.axis_size("dp")
    shards = lax.axis_size("seq")
    heads = decay_log.shape[0]
    head_width = full // heads
    runs = tokens // SEG
    capacity = runs // groups + 1
    pad = LANES - heads

    own = source_rows[0].reshape(runs, SEG)[:, 0][None, :] // SEG
    wanted = lax.all_to_all(
        jnp.broadcast_to(own, (groups, runs)), "dp", split_axis=0, concat_axis=0, tiled=True
    )
    me = lax.axis_index("dp").astype(jnp.int32)[None]
    send, pick = make_plan(groups, shards, runs, capacity, me, wanted, own)

    small = jnp.concatenate([key_rows, query_rows, jnp.pad(step_rows, ((0, 0), (0, pad)))], axis=1)
    small = small.reshape(runs, SEG, 3 * LANES)
    values = token_rows.reshape(runs, SEG, full)

    def exchange(block):
        got = lax.all_to_all(block, "dp", split_axis=0, concat_axis=0, tiled=True)
        return got.reshape(groups * capacity, SEG, block.shape[-1])

    small_sent = collect(send, small, send, groups, capacity, 0, 3 * LANES)
    small_got = exchange(small_sent)

    chunk = CHUNK_HEADS
    count = heads // chunk
    width = chunk * head_width
    sent = []
    got = []
    for number in range(count):
        if number == 0:
            token = small_sent
        elif number == 1:
            token = sent[0]
        else:
            token = got[number - 2]
        block = collect(send, values, token, groups, capacity, number * width, width)
        sent.append(block)
        got.append(exchange(block))

    starts = document_starts[0] - lax.axis_index("seq").astype(jnp.int32) * tokens
    decay = jnp.pad(decay_log, (0, pad))[None, :]
    prepared = prepare(pick, starts, small_got, decay, tokens)
    cum, bias, entry, end, device, through, keys, query, scores = prepared
    lane_head = jnp.arange(full) // head_width
    ones = (jnp.arange(2 * LANES)[:, None] % LANES == lane_head[None, :]).astype(bf16)
    through = jnp.repeat(through[0, :heads], head_width)[None, :]
    skip = jnp.repeat(skip_gain, head_width)[None, :]

    incoming = []
    for number in range(count):
        part = slice(number * width, (number + 1) * width)
        final = final_state(pick, got[number], keys, device, ones[:, part], tokens)
        entering = jnp.zeros_like(final)
        for hop in range(shards - 1):
            outgoing = through[:, part] * entering + final
            entering = shifted(outgoing.astype(bf16), "seq", 1).astype(f32)
        incoming.append(entering)

    result = None
    for number in range(count):
        part = slice(number * width, (number + 1) * width)
        result = layer(
            result, pick, got[number], (cum, bias, entry, end, keys, query, scores),
            ones[:, part], skip[:, part], incoming[number], tokens, full, number * width,
            number * chunk, chunk,
        )
    return result[None]


def solution(mesh):
    in_specs = (
        P(("dp", "seq"), None),
        P(("dp", "seq"), None),
        P(("dp", "seq"), None),
        P(("dp", "seq"), None),
        P(),
        P(),
        P("dp", "seq"),
        P("dp", None),
    )
    out_specs = P("dp", "seq", None)
    return jax.shard_map(
        on_device, mesh=mesh, in_specs=in_specs, out_specs=out_specs, check_vma=False
    )
```

profile of v0, /device:TPU:0, one launch (start us, length us, event | category | flops | bytes accessed | tf_op | source)
XLA Modules:
  0.0 351.3 jit_solution(9604888761089013167)
XLA Ops:
  1.5 5.2 %all-to-all-start = ((s32[8,1,160]{2,1,0:T(1,128)}), s32[8,1,160]{2,1,0:T(1,128)S(1)}, u32[]{:S(2)}, u32[]{:S(2)}) async-start(s32[8,1,160]{2,1,0:T(1,128)} %broadcast_in_dim.23), calls=%async_computation | async-start | bytes 16384 | tf_op jit(solution)/shard_map/all_to_all | solution.py:414
  12.5 1.6 plan.1
  14.1 3.6 %collect.6.token_ref = bf16[8,21,8,384]{3,2,1,0:T(8,128)(2,1)} custom-call(s32[8,128]{1,0:T(8,128)} %get-tuple-element.17.send_ref.token_ref, bf16[160,8,384]{2,1,0:T(8,128)(2,1)} %bitcast.40, s32[8,128]{1,0:T(8,128)} %get-tuple-element.17.send_ref.token_ref), custom_call_target="tpu_custom_call" | custom-call | bytes 2064384 | tf_op jit(solution)/shard_map/collect/pallas_call | solution.py:110
  17.7 4.2 %all-to-all-start.4 = ((bf16[8,21,8,384]{3,2,1,0:T(8,128)(2,1)}), bf16[8,21,8,384]{3,2,1,0:T(8,128)(2,1)S(1)}, u32[]{:S(2)}, u32[]{:S(2)}) async-start(bf16[8,21,8,384]{3,2,1,0:T(8,128)(2,1)} %collect.6.token_ref), calls=%async_computation.4 | async-start | bytes 2064384 | tf_op jit(solution)/shard_map/all_to_all | solution.py:425
  21.9 3.9 %collect.7.token_ref = bf16[8,21,8,1024]{3,2,1,0:T(8,128)(2,1)} custom-call(s32[8,128]{1,0:T(8,128)} %get-tuple-element.17.send_ref.token_ref, bf16[160,8,5120]{2,1,0:T(8,128)(2,1)} %bitcast.26, bf16[8,21,8,384]{3,2,1,0:T(8,128)(2,1)} %collect.6.token_ref), custom_call_target="tpu_custom_call" | custom-call | bytes 5505024 | tf_op jit(solution)/shard_map/collect/pallas_call | solution.py:110
  25.8 11.3 %all-to-all-done.4 = bf16[8,21,8,384]{3,2,1,0:T(8,128)(2,1)S(1)} async-done(((bf16[8,21,8,384]{3,2,1,0:T(8,128)(2,1)}), bf16[8,21,8,384]{3,2,1,0:T(8,128)(2,1)S(1)}, u32[]{:S(2)}, u32[]{:S(2)}) %all-to-all-start.4) | async-done | bytes 1032224 | tf_op jit(solution)/shard_map/all_to_all | solution.py:425
  38.1 3.6 %all-to-all-start.1 = ((bf16[8,21,8,1024]{3,2,1,0:T(8,128)(2,1)}), bf16[8,21,8,1024]{3,2,1,0:T(8,128)(2,1)S(1)}, u32[]{:S(2)}, u32[]{:S(2)}) async-start(bf16[8,21,8,1024]{3,2,1,0:T(8,128)(2,1)} %collect.7.token_ref), calls=%async_computation.1 | async-start | bytes 5505024 | tf_op jit(solution)/shard_map/all_to_all | solution.py:425
  41.7 3.9 %collect.10 = bf16[8,21,8,1024]{3,2,1,0:T(8,128)(2,1)} custom-call(s32[8,128]{1,0:T(8,128)} %get-tuple-element.17.send_ref.token_ref, bf16[160,8,5120]{2,1,0:T(8,128)(2,1)} %bitcast.27, bf16[8,21,8,1024]{3,2,1,0:T(8,128)(2,1)} %collect.7.token_ref), custom_call_target="tpu_custom_call" | custom-call | bytes 5505024 | tf_op jit(solution)/shard_map/collect/pallas_call | solution.py:110
  45.6 29.7 %all-to-all-done.1 = bf16[8,21,8,1024]{3,2,1,0:T(8,128)(2,1)S(1)} async-done(((bf16[8,21,8,1024]{3,2,1,0:T(8,128)(2,1)}), bf16[8,21,8,1024]{3,2,1,0:T(8,128)(2,1)S(1)}, u32[]{:S(2)}, u32[]{:S(2)}) %all-to-all-start.1) | async-done | bytes 2752544 | tf_op jit(solution)/shard_map/all_to_all | solution.py:425
  76.8 4.5 %all-to-all-start.5 = ((bf16[8,21,8,1024]{3,2,1,0:T(8,128)(2,1)}), bf16[8,21,8,1024]{3,2,1,0:T(8,128)(2,1)}, u32[]{:S(2)}, u32[]{:S(2)}) async-start(bf16[8,21,8,1024]{3,2,1,0:T(8,128)(2,1)} %collect.10), calls=%async_computation.5 | async-start | bytes 5505024 | tf_op jit(solution)/shard_map/all_to_all | solution.py:425
  81.3 3.9 %collect.8 = bf16[8,21,8,1024]{3,2,1,0:T(8,128)(2,1)} custom-call(s32[8,128]{1,0:T(8,128)} %get-tuple-element.17.send_ref.token_ref, bf16[160,8,5120]{2,1,0:T(8,128)(2,1)} %bitcast.28, bf16[168,8,1024]{2,1,0:T(8,128)(2,1)} %bitcast.31), custom_call_target="tpu_custom_call" | custom-call | bytes 5505024 | tf_op jit(solution)/shard_map/collect/pallas_call | solution.py:110
  85.2 29.7 %all-to-all-done.5 = bf16[8,21,8,1024]{3,2,1,0:T(8,128)(2,1)} async-done(((bf16[8,21,8,1024]{3,2,1,0:T(8,128)(2,1)}), bf16[8,21,8,1024]{3,2,1,0:T(8,128)(2,1)}, u32[]{:S(2)}, u32[]{:S(2)}) %all-to-all-start.5) | async-done | bytes 2752544 | tf_op jit(solution)/shard_map/all_to_all | solution.py:425
  114.9 3.6 %all-to-all-start.2 = ((bf16[8,21,8,1024]{3,2,1,0:T(8,128)(2,1)}), bf16[8,21,8,1024]{3,2,1,0:T(8,128)(2,1)S(1)}, u32[]{:S(2)}, u32[]{:S(2)}) async-start(bf16[8,21,8,1024]{3,2,1,0:T(8,128)(2,1)} %collect.8), calls=%async_computation.2 | async-start | bytes 5505024 | tf_op jit(solution)/shard_map/all_to_all | solution.py:425
  119.1 2.1 compare_convert_fusion
  121.2 3.9 %collect.11 = bf16[8,21,8,1024]{3,2,1,0:T(8,128)(2,1)} custom-call(s32[8,128]{1,0:T(8,128)} %get-tuple-element.17.send_ref.token_ref, bf16[160,8,5120]{2,1,0:T(8,128)(2,1)} %bitcast.29, bf16[168,8,1024]{2,1,0:T(8,128)(2,1)} %bitcast.12.token_ref.values_ref), custom_call_target="tpu_custom_call" | custom-call | bytes 5505024 | tf_op jit(solution)/shard_map/collect/pallas_call | solution.py:110
  125.1 27.0 %all-to-all-done.2 = bf16[8,21,8,1024]{3,2,1,0:T(8,128)(2,1)S(1)} async-done(((bf16[8,21,8,1024]{3,2,1,0:T(8,128)(2,1)}), bf16[8,21,8,1024]{3,2,1,0:T(8,128)(2,1)S(1)}, u32[]{:S(2)}, u32[]{:S(2)}) %all-to-all-start.2) | async-done | bytes 2752544 | tf_op jit(solution)/shard_map/all_to_all | solution.py:425
  152.2 1.6 copy-done.1
  153.8 4.4 %all-to-all-start.6 = ((bf16[8,21,8,1024]{3,2,1,0:T(8,128)(2,1)}), bf16[8,21,8,1024]{3,2,1,0:T(8,128)(2,1)}, u32[]{:S(2)}, u32[]{:S(2)}) async-start(bf16[8,21,8,1024]{3,2,1,0:T(8,128)(2,1)} %collect.11), calls=%async_computation.6 | async-start | bytes 5505024 | tf_op jit(solution)/shard_map/all_to_all | solution.py:425
  158.9 3.2 fusion.5
  162.2 8.5 %prepare.1 = (f32[1280,128]{1,0:T(8,128)}, f32[128,1280]{1,0:T(8,128)}, bf16[1280,256]{1,0:T(8,128)(2,1)}, bf16[1280,256]{1,0:T(8,128)(2,1)}, bf16[1280,256]{1,0...) custom-call(s32[160]{0:T(256)} %bitcast.41, ...), custom_call_target="tpu_custom_call" | custom-call | tf_op jit(solution)/shard_map/prepare/pallas_call | solution.py:227
  171.4 7.7 %final_state.9 = f32[128,1024]{1,0:T(8,128)} custom-call(s32[160]{0:T(256)} %bitcast.42, bf16[168,8,1024]{2,1,0:T(8,128)(2,1)} %bitcast.32, bf16[128,1280]{1,0:T(8,128)(2,1)} %get-tuple-element.22.keys_ref, bf16[1280,256]{1,0:T(8,128)(2,1)} %get-tuple-element.26.device_ref, bf16[256,1024]{1,0:T(8,128)(2,1)} %get-tuple-element.27.ones_ref), custom_call_target="tpu_custom_call" | custom-call | flops 1006632960 | bytes 2621440 | tf_op jit(solution)/shard_map/final_state/pallas_call | solution.py:282
  180.2 3.5 collective-permute-start.12
  183.7 7.8 %final_state.8 = f32[128,1024]{1,0:T(8,128)} custom-call(s32[160]{0:T(256)} %bitcast.43, bf16[168,8,1024]{2,1,0:T(8,128)(2,1)} %bitcast.12.token_ref.values_ref, bf16[128,1280]{1,0:T(8,128)(2,1)} %get-tuple-element.22.keys_ref, bf16[1280,256]{1,0:T(8,128)(2,1)} %get-tuple-element.26.device_ref, bf16[256,1024]{1,0:T(8,128)(2,1)} %get-tuple-element.28.ones_ref), custom_call_target="tpu_custom_call" | custom-call | flops 1006632960 | bytes 2621440 | tf_op jit(solution)/shard_map/final_state/pallas_call | solution.py:282
  192.7 4.2 %collective-permute-start.9 = (bf16[128,1024]{1,0:T(8,128)(2,1)S(1)}, bf16[128,1024]{1,0:T(8,128)(2,1)}, u32[]{:S(2)}, u32[]{:S(2)}) collective-permute-start(bf16[128,1024]{1,0:T(8,128)(2,1)S(1)} %add_convert_fusion.5), channel_id=1, source_target_pairs={{0,1},{1,2},{2,3},{4,5},{5,6},{6,7},{8,9},{9,10},{10,11},{12,13},{... | collective-permute-start | bytes 786440 | tf_op jit(solution)/shard_map/ppermute | solution.py:398
  198.3 3.5 collective-permute-start.13
  201.7 3.9 %collect.9 = bf16[8,21,8,1024]{3,2,1,0:T(8,128)(2,1)} custom-call(s32[8,128]{1,0:T(8,128)} %get-tuple-element.17.send_ref.token_ref, bf16[160,8,5120]{2,1,0:T(8,128)(2,1)} %bitcast.30, bf16[168,8,1024]{2,1,0:T(8,128)(2,1)} %bitcast.34), custom_call_target="tpu_custom_call" | custom-call | bytes 5505024 | tf_op jit(solution)/shard_map/collect/pallas_call | solution.py:110
  205.7 4.2 %all-to-all-start.3 = ((bf16[8,21,8,1024]{3,2,1,0:T(8,128)(2,1)}), bf16[8,21,8,1024]{3,2,1,0:T(8,128)(2,1)S(1)}, u32[]{:S(2)}, u32[]{:S(2)}) async-start(bf16[8,21,8,1024]{3,2,1,0:T(8,128)(2,1)} %collect.9), calls=%async_computation.3 | async-start | bytes 5505024 | tf_op jit(solution)/shard_map/all_to_all | solution.py:425
  213.5 1.8 collective-permute-start.14
  215.4 3.6 %collective-permute-done.10 = bf16[128,1024]{1,0:T(8,128)(2,1)S(1)} collective-permute-done((bf16[128,1024]{1,0:T(8,128)(2,1)S(1)}, bf16[128,1024]{1,0:T(8,128)(2,1)S(1)}, u32[]{:S(2)}, u32[]{:S(2)}) %collective-permute-start.10) | collective-permute-done | bytes 262176 | tf_op jit(solution)/shard_map/ppermute | solution.py:398
  219.0 4.4 %collective-permute-start.11 = (bf16[128,1024]{1,0:T(8,128)(2,1)S(1)}, bf16[128,1024]{1,0:T(8,128)(2,1)S(1)}, u32[]{:S(2)}, u32[]{:S(2)}) collective-permute-start(bf16[128,1024]{1,0:T(8,128)(2,1)S(1)} %add_convert_fusion.3), channel_id=1, source_target_pairs={{0,1},{1,2},{2,3},{4,5},{5,6},{6,7},{8,9},{9,10},{10,11},{12,13},{... | collective-permute-start | bytes 786440 | tf_op jit(solution)/shard_map/ppermute | solution.py:398
  225.4 4.6 %collective-permute-done.11 = bf16[128,1024]{1,0:T(8,128)(2,1)S(1)} collective-permute-done((bf16[128,1024]{1,0:T(8,128)(2,1)S(1)}, bf16[128,1024]{1,0:T(8,128)(2,1)S(1)}, u32[]{:S(2)}, u32[]{:S(2)}) %collective-permute-start.11) | collective-permute-done | bytes 262176 | tf_op jit(solution)/shard_map/ppermute | solution.py:398
  230.9 12.6 %layer.5.rest_0_ = bf16[1280,5120]{1,0:T(8,128)(2,1)} custom-call(s32[160]{0:T(256)} %bitcast.44, bf16[168,8,1024]{2,1,0:T(8,128)(2,1)} %bitcast.33, f32[1280,128]{1,0:T(8,128)} %get-tuple-element.18.cum_ref, f32[128,1280]{1,0:T(8,128)} %get-tuple-element.19.bias_ref, bf16[1280,256]{1,0:T(8,128)(2,1)} %get-tuple-element.20.entry_ref, ...), custom_call_target="tpu_custom_call" | custom-call | flops 2684354560 | bytes 5242880 | tf_op jit(solution)/shard_map/layer/pallas_call | solution.py:368
  243.5 7.7 %final_state.7 = f32[128,1024]{1,0:T(8,128)} custom-call(s32[160]{0:T(256)} %bitcast.45, bf16[168,8,1024]{2,1,0:T(8,128)(2,1)} %bitcast.35, bf16[128,1280]{1,0:T(8,128)(2,1)} %get-tuple-element.22.keys_ref, bf16[1280,256]{1,0:T(8,128)(2,1)} %get-tuple-element.26.device_ref, bf16[256,1024]{1,0:T(8,128)(2,1)} %get-tuple-element.29.ones_ref), custom_call_target="tpu_custom_call" | custom-call | flops 1006632960 | bytes 2621440 | tf_op jit(solution)/shard_map/final_state/pallas_call | solution.py:282
  252.3 4.4 %collective-permute-start.6 = (bf16[128,1024]{1,0:T(8,128)(2,1)S(1)}, bf16[128,1024]{1,0:T(8,128)(2,1)S(1)}, u32[]{:S(2)}, u32[]{:S(2)}) collective-permute-start(bf16[128,1024]{1,0:T(8,128)(2,1)S(1)} %add_convert_fusion.8), channel_id=1, source_target_pairs={{0,1},{1,2},{2,3},{4,5},{5,6},{6,7},{8,9},{9,10},{10,11},{12,13},{... | collective-permute-start | bytes 786440 | tf_op jit(solution)/shard_map/ppermute | solution.py:398
  256.7 7.8 %final_state.6 = f32[128,1024]{1,0:T(8,128)} custom-call(s32[160]{0:T(256)} %bitcast.46, bf16[168,8,1024]{2,1,0:T(8,128)(2,1)} %bitcast.13.values_ref, bf16[128,1280]{1,0:T(8,128)(2,1)} %get-tuple-element.22.keys_ref, bf16[1280,256]{1,0:T(8,128)(2,1)} %get-tuple-element.26.device_ref, bf16[256,1024]{1,0:T(8,128)(2,1)} %get-tuple-element.30.ones_ref), custom_call_target="tpu_custom_call" | custom-call | flops 1006632960 | bytes 2621440 | tf_op jit(solution)/shard_map/final_state/pallas_call | solution.py:282
  265.6 2.6 collective-permute-start.3
  269.0 2.0 collective-permute-start.7
  271.0 1.5 copy-done.2
  272.5 7.8 %final_state.5 = f32[128,1024]{1,0:T(8,128)} custom-call(s32[160]{0:T(256)} %bitcast.47, bf16[168,8,1024]{2,1,0:T(8,128)(2,1)} %bitcast.37, bf16[128,1280]{1,0:T(8,128)(2,1)} %get-tuple-element.22.keys_ref, bf16[1280,256]{1,0:T(8,128)(2,1)} %get-tuple-element.26.device_ref, bf16[256,1024]{1,0:T(8,128)(2,1)} %get-tuple-element.31.ones_ref), custom_call_target="tpu_custom_call" | custom-call | flops 1006632960 | bytes 2621440 | tf_op jit(solution)/shard_map/final_state/pallas_call | solution.py:282
  283.9 1.8 collective-permute-start.4
  286.7 1.9 collective-permute-start.8
  289.6 4.6 %collective-permute-start.1 = (bf16[128,1024]{1,0:T(8,128)(2,1)S(1)}, bf16[128,1024]{1,0:T(8,128)(2,1)S(1)}, u32[]{:S(2)}, u32[]{:S(2)}) collective-permute-start(bf16[128,1024]{1,0:T(8,128)(2,1)S(1)} %add_convert_fusion.13), channel_id=1, source_target_pairs={{0,1},{1,2},{2,3},{4,5},{5,6},{6,7},{8,9},{9,10},{10,11},{12,13},{... | collective-permute-start | bytes 786440 | tf_op jit(solution)/shard_map/ppermute | solution.py:398
  294.2 12.6 %layer.6.rest_0_ = bf16[1280,5120]{1,0:T(8,128)(2,1)} custom-call(s32[160]{0:T(256)} %bitcast.48, bf16[168,8,1024]{2,1,0:T(8,128)(2,1)} %bitcast.12.token_ref.values_ref, f32[1280,128]{1,0:T(8,128)} %get-tuple-element.18.cum_ref, f32[128,1280]{1,0:T(8,128)} %get-tuple-element.19.bias_ref, ...), custom_call_target="tpu_custom_call", output_to_operand_aliasing={{}: (12, {})} | custom-call | flops 2684354560 | bytes 5242880 | tf_op jit(solution)/shard_map/layer/pallas_call | solution.py:368
  306.8 1.9 collective-permute-start.5
  309.7 1.9 collective-permute-start.2
  311.6 12.6 %layer.7.rest_0_ = bf16[1280,5120]{1,0:T(8,128)(2,1)} custom-call(s32[160]{0:T(256)} %bitcast.49, bf16[168,8,1024]{2,1,0:T(8,128)(2,1)} %bitcast.36, f32[1280,128]{1,0:T(8,128)} %get-tuple-element.18.cum_ref, f32[128,1280]{1,0:T(8,128)} %get-tuple-element.19.bias_ref, ...), custom_call_target="tpu_custom_call", output_to_operand_aliasing={{}: (12, {})} | custom-call | flops 2684354560 | bytes 5242880 | tf_op jit(solution)/shard_map/layer/pallas_call | solution.py:368
  325.1 12.6 %layer.8.rest_0_ = bf16[1280,5120]{1,0:T(8,128)(2,1)} custom-call(s32[160]{0:T(256)} %bitcast.50, bf16[168,8,1024]{2,1,0:T(8,128)(2,1)} %bitcast.13.values_ref, f32[1280,128]{1,0:T(8,128)} %get-tuple-element.18.cum_ref, f32[128,1280]{1,0:T(8,128)} %get-tuple-element.19.bias_ref, ...), custom_call_target="tpu_custom_call", output_to_operand_aliasing={{}: (12, {})} | custom-call | flops 2684354560 | bytes 5242880 | tf_op jit(solution)/shard_map/layer/pallas_call | solution.py:368
  338.6 12.6 %layer.9 = bf16[1280,5120]{1,0:T(8,128)(2,1)} custom-call(s32[160]{0:T(256)} %bitcast.51, bf16[168,8,1024]{2,1,0:T(8,128)(2,1)} %bitcast.38, f32[1280,128]{1,0:T(8,128)} %get-tuple-element.18.cum_ref, f32[128,1280]{1,0:T(8,128)} %get-tuple-element.19.bias_ref, bf16[1280,256]{1,0:T(8,128)(2,1)} %get-tuple-element.20.entry_ref, ...), custom_call_target="tpu_custom_call", output_to_operand_aliasing={{}: (12, {})} | custom-call | flops 2684354560 | bytes 5242880 | tf_op jit(solution)/shard_map/layer/pallas_call | solution.py:368
  (89 shorter events, 32.9 us)
Async XLA Ops:
  1.5 10.3 %all-to-all-start = ((s32[8,1,160]{2,1,0:T(1,128)}), s32[8,1,160]{2,1,0:T(1,128)S(1)}, u32[]{:S(2)}, u32[]{:S(2)}) async-start(s32[8,1,160]{2,1,0:T(1,128)} %broadcast_in_dim.23), calls=%async_computation | async-start | bytes 16384 | tf_op jit(solution)/shard_map/all_to_all | solution.py:414
  17.7 19.4 %all-to-all-start.4 = ((bf16[8,21,8,384]{3,2,1,0:T(8,128)(2,1)}), bf16[8,21,8,384]{3,2,1,0:T(8,128)(2,1)S(1)}, u32[]{:S(2)}, u32[]{:S(2)}) async-start(bf16[8,21,8,384]{3,2,1,0:T(8,128)(2,1)} %collect.6.token_ref), calls=%async_computation.4 | async-start | bytes 2064384 | tf_op jit(solution)/shard_map/all_to_all | solution.py:425
  37.1 1.0 copy-start.8
  38.1 37.2 %all-to-all-start.1 = ((bf16[8,21,8,1024]{3,2,1,0:T(8,128)(2,1)}), bf16[8,21,8,1024]{3,2,1,0:T(8,128)(2,1)S(1)}, u32[]{:S(2)}, u32[]{:S(2)}) async-start(bf16[8,21,8,1024]{3,2,1,0:T(8,128)(2,1)} %collect.7.token_ref), calls=%async_computation.1 | async-start | bytes 5505024 | tf_op jit(solution)/shard_map/all_to_all | solution.py:425
  75.3 1.5 copy-start
  76.8 38.1 %all-to-all-start.5 = ((bf16[8,21,8,1024]{3,2,1,0:T(8,128)(2,1)}), bf16[8,21,8,1024]{3,2,1,0:T(8,128)(2,1)}, u32[]{:S(2)}, u32[]{:S(2)}) async-start(bf16[8,21,8,1024]{3,2,1,0:T(8,128)(2,1)} %collect.10), calls=%async_computation.5 | async-start | bytes 5505024 | tf_op jit(solution)/shard_map/all_to_all | solution.py:425
  85.2 33.4 %copy-start.11 = (s32[1,6]{1,0:T(1,128)S(1)}, s32[1,6]{1,0:T(1,128)}, u32[]{:S(2)}) copy-start(s32[1,6]{1,0:T(1,128)} %param.15) | copy-start | bytes 76
  114.9 37.2 %all-to-all-start.2 = ((bf16[8,21,8,1024]{3,2,1,0:T(8,128)(2,1)}), bf16[8,21,8,1024]{3,2,1,0:T(8,128)(2,1)S(1)}, u32[]{:S(2)}, u32[]{:S(2)}) async-start(bf16[8,21,8,1024]{3,2,1,0:T(8,128)(2,1)} %collect.8), calls=%async_computation.2 | async-start | bytes 5505024 | tf_op jit(solution)/shard_map/all_to_all | solution.py:425
  125.1 33.1 %copy-start.12 = (f32[80]{0:T(128)S(1)}, f32[80]{0:T(128)}, u32[]{:S(2)}) copy-start(f32[80]{0:T(128)} %param.12) | copy-start | bytes 964
  125.1 33.6 %copy-start.10 = (f32[80]{0:T(128)S(1)}, f32[80]{0:T(128)}, u32[]{:S(2)}) copy-start(f32[80]{0:T(128)} %param.13) | copy-start | bytes 964
  152.2 1.6 copy-start.1
  153.8 51.9 %all-to-all-start.6 = ((bf16[8,21,8,1024]{3,2,1,0:T(8,128)(2,1)}), bf16[8,21,8,1024]{3,2,1,0:T(8,128)(2,1)}, u32[]{:S(2)}, u32[]{:S(2)}) async-start(bf16[8,21,8,1024]{3,2,1,0:T(8,128)(2,1)} %collect.11), calls=%async_computation.6 | async-start | bytes 5505024 | tf_op jit(solution)/shard_map/all_to_all | solution.py:425
  171.4 26.1 %copy-start.9 = (f32[1,1024]{1,0:T(1,128)}, f32[1,1024]{1,0:T(1,128)S(1)}, u32[]{:S(2)}) copy-start(f32[1,1024]{1,0:T(1,128)S(1)} %get-tuple-element.32) | copy-start | bytes 12292
  180.2 17.2 %collective-permute-start.12 = (bf16[128,1024]{1,0:T(8,128)(2,1)S(1)}, bf16[128,1024]{1,0:T(8,128)(2,1)S(1)}, u32[]{:S(2)}, u32[]{:S(2)}) collective-permute-start(bf16[128,1024]{1,0:T(8,128)(2,1)S(1)} %add_convert_fusion.2), channel_id=1, source_target_pairs={{0,1},{1,2},{2,3},{4,5},{5,6},{6,7},{8,9},{9,10},{10,11},{12,13},{... | collective-permute-start | bytes 786440 | tf_op jit(solution)/shard_map/ppermute | solution.py:398
  183.7 13.7 %copy-start.6 = (f32[128,1024]{1,0:T(8,128)S(1)}, f32[128,1024]{1,0:T(8,128)}, u32[]{:S(2)}) copy-start(f32[128,1024]{1,0:T(8,128)} %final_state.9) | copy-start | bytes 1572868
  192.7 17.3 %collective-permute-start.9 = (bf16[128,1024]{1,0:T(8,128)(2,1)S(1)}, bf16[128,1024]{1,0:T(8,128)(2,1)}, u32[]{:S(2)}, u32[]{:S(2)}) collective-permute-start(bf16[128,1024]{1,0:T(8,128)(2,1)S(1)} %add_convert_fusion.5), channel_id=1, source_target_pairs={{0,1},{1,2},{2,3},{4,5},{5,6},{6,7},{8,9},{9,10},{10,11},{12,13},{... | collective-permute-start | bytes 786440 | tf_op jit(solution)/shard_map/ppermute | solution.py:398
  198.3 14.0 %collective-permute-start.13 = (bf16[128,1024]{1,0:T(8,128)(2,1)}, bf16[128,1024]{1,0:T(8,128)(2,1)}, u32[]{:S(2)}, u32[]{:S(2)}) collective-permute-start(bf16[128,1024]{1,0:T(8,128)(2,1)} %add_convert_fusion.1), channel_id=1, source_target_pairs={{0,1},{1,2},{2,3},{4,5},{5,6},{6,7},{8,9},{9,10},{10,11},{12,13},{... | collective-permute-start | bytes 786440 | tf_op jit(solution)/shard_map/ppermute | solution.py:398
  205.7 4.3 %copy-start.5 = (f32[128,1024]{1,0:T(8,128)S(1)}, f32[128,1024]{1,0:T(8,128)}, u32[]{:S(2)}) copy-start(f32[128,1024]{1,0:T(8,128)} %final_state.8) | copy-start | bytes 1572868
  205.7 65.3 %all-to-all-start.3 = ((bf16[8,21,8,1024]{3,2,1,0:T(8,128)(2,1)}), bf16[8,21,8,1024]{3,2,1,0:T(8,128)(2,1)S(1)}, u32[]{:S(2)}, u32[]{:S(2)}) async-start(bf16[8,21,8,1024]{3,2,1,0:T(8,128)(2,1)} %collect.9), calls=%async_computation.3 | async-start | bytes 5505024 | tf_op jit(solution)/shard_map/all_to_all | solution.py:425
  211.0 8.0 %collective-permute-start.10 = (bf16[128,1024]{1,0:T(8,128)(2,1)S(1)}, bf16[128,1024]{1,0:T(8,128)(2,1)S(1)}, u32[]{:S(2)}, u32[]{:S(2)}) collective-permute-start(bf16[128,1024]{1,0:T(8,128)(2,1)S(1)} %add_convert_fusion.4), channel_id=1, source_target_pairs={{0,1},{1,2},{2,3},{4,5},{5,6},{6,7},{8,9},{9,10},{10,11},{12,13},{... | collective-permute-start | bytes 786440 | tf_op jit(solution)/shard_map/ppermute | solution.py:398
  213.5 11.1 %collective-permute-start.14 = (bf16[128,1024]{1,0:T(8,128)(2,1)S(1)}, bf16[128,1024]{1,0:T(8,128)(2,1)S(1)}, u32[]{:S(2)}, u32[]{:S(2)}) collective-permute-start(bf16[128,1024]{1,0:T(8,128)(2,1)S(1)} %add_convert_fusion), channel_id=1, source_target_pairs={{0,1},{1,2},{2,3},{4,5},{5,6},{6,7},{8,9},{9,10},{10,11},{12,13},{... | collective-permute-start | bytes 786440 | tf_op jit(solution)/shard_map/ppermute | solution.py:398
  219.0 11.0 %collective-permute-start.11 = (bf16[128,1024]{1,0:T(8,128)(2,1)S(1)}, bf16[128,1024]{1,0:T(8,128)(2,1)S(1)}, u32[]{:S(2)}, u32[]{:S(2)}) collective-permute-start(bf16[128,1024]{1,0:T(8,128)(2,1)S(1)} %add_convert_fusion.3), channel_id=1, source_target_pairs={{0,1},{1,2},{2,3},{4,5},{5,6},{6,7},{8,9},{9,10},{10,11},{12,13},{... | collective-permute-start | bytes 786440 | tf_op jit(solution)/shard_map/ppermute | solution.py:398
  252.3 15.9 %collective-permute-start.6 = (bf16[128,1024]{1,0:T(8,128)(2,1)S(1)}, bf16[128,1024]{1,0:T(8,128)(2,1)S(1)}, u32[]{:S(2)}, u32[]{:S(2)}) collective-permute-start(bf16[128,1024]{1,0:T(8,128)(2,1)S(1)} %add_convert_fusion.8), channel_id=1, source_target_pairs={{0,1},{1,2},{2,3},{4,5},{5,6},{6,7},{8,9},{9,10},{10,11},{12,13},{... | collective-permute-start | bytes 786440 | tf_op jit(solution)/shard_map/ppermute | solution.py:398
  256.7 11.5 %copy-start.7 = (f32[128,1024]{1,0:T(8,128)S(1)}, f32[128,1024]{1,0:T(8,128)}, u32[]{:S(2)}) copy-start(f32[128,1024]{1,0:T(8,128)} %final_state.7) | copy-start | bytes 1572868
  265.6 17.2 %collective-permute-start.3 = (bf16[128,1024]{1,0:T(8,128)(2,1)S(1)}, bf16[128,1024]{1,0:T(8,128)(2,1)}, u32[]{:S(2)}, u32[]{:S(2)}) collective-permute-start(bf16[128,1024]{1,0:T(8,128)(2,1)S(1)} %add_convert_fusion.11), channel_id=1, source_target_pairs={{0,1},{1,2},{2,3},{4,5},{5,6},{6,7},{8,9},{9,10},{10,11},{12,13},{... | collective-permute-start | bytes 786440 | tf_op jit(solution)/shard_map/ppermute | solution.py:398
  269.0 16.7 %collective-permute-start.7 = (bf16[128,1024]{1,0:T(8,128)(2,1)}, bf16[128,1024]{1,0:T(8,128)(2,1)}, u32[]{:S(2)}, u32[]{:S(2)}) collective-permute-start(bf16[128,1024]{1,0:T(8,128)(2,1)} %add_convert_fusion.7), channel_id=1, source_target_pairs={{0,1},{1,2},{2,3},{4,5},{5,6},{6,7},{8,9},{9,10},{10,11},{12,13},{... | collective-permute-start | bytes 786440 | tf_op jit(solution)/shard_map/ppermute | solution.py:398
  271.0 1.5 copy-start.2
  272.5 10.3 %copy-start.3 = (f32[128,1024]{1,0:T(8,128)S(1)}, f32[128,1024]{1,0:T(8,128)}, u32[]{:S(2)}) copy-start(f32[128,1024]{1,0:T(8,128)} %final_state.6) | copy-start | bytes 1572868
  280.4 9.1 %copy-start.4 = (f32[128,1024]{1,0:T(8,128)S(1)}, f32[128,1024]{1,0:T(8,128)}, u32[]{:S(2)}) copy-start(f32[128,1024]{1,0:T(8,128)} %final_state.5) | copy-start | bytes 1572868
  281.5 8.0 %collective-permute-start = (bf16[128,1024]{1,0:T(8,128)(2,1)S(1)}, bf16[128,1024]{1,0:T(8,128)(2,1)S(1)}, u32[]{:S(2)}, u32[]{:S(2)}) collective-permute-start(bf16[128,1024]{1,0:T(8,128)(2,1)S(1)} %add_convert_fusion.14), channel_id=1, source_target_pairs={{0,1},{1,2},{2,3},{4,5},{5,6},{6,7},{8,9},{9,10},{10,11},{12,13},{... | collective-permute-start | bytes 786440 | tf_op jit(solution)/shard_map/ppermute | solution.py:398
  283.9 22.9 %collective-permute-start.4 = (bf16[128,1024]{1,0:T(8,128)(2,1)S(1)}, bf16[128,1024]{1,0:T(8,128)(2,1)S(1)}, u32[]{:S(2)}, u32[]{:S(2)}) collective-permute-start(bf16[128,1024]{1,0:T(8,128)(2,1)S(1)} %add_convert_fusion.10), channel_id=1, source_target_pairs={{0,1},{1,2},{2,3},{4,5},{5,6},{6,7},{8,9},{9,10},{10,11},{12,13},{... | collective-permute-start | bytes 786440 | tf_op jit(solution)/shard_map/ppermute | solution.py:398
  286.7 22.0 %collective-permute-start.8 = (bf16[128,1024]{1,0:T(8,128)(2,1)S(1)}, bf16[128,1024]{1,0:T(8,128)(2,1)S(1)}, u32[]{:S(2)}, u32[]{:S(2)}) collective-permute-start(bf16[128,1024]{1,0:T(8,128)(2,1)S(1)} %add_convert_fusion.6), channel_id=1, source_target_pairs={{0,1},{1,2},{2,3},{4,5},{5,6},{6,7},{8,9},{9,10},{10,11},{12,13},{... | collective-permute-start | bytes 786440 | tf_op jit(solution)/shard_map/ppermute | solution.py:398
  289.6 20.1 %collective-permute-start.1 = (bf16[128,1024]{1,0:T(8,128)(2,1)S(1)}, bf16[128,1024]{1,0:T(8,128)(2,1)S(1)}, u32[]{:S(2)}, u32[]{:S(2)}) collective-permute-start(bf16[128,1024]{1,0:T(8,128)(2,1)S(1)} %add_convert_fusion.13), channel_id=1, source_target_pairs={{0,1},{1,2},{2,3},{4,5},{5,6},{6,7},{8,9},{9,10},{10,11},{12,13},{... | collective-permute-start | bytes 786440 | tf_op jit(solution)/shard_map/ppermute | solution.py:398
  306.8 17.4 %collective-permute-start.5 = (bf16[128,1024]{1,0:T(8,128)(2,1)S(1)}, bf16[128,1024]{1,0:T(8,128)(2,1)S(1)}, u32[]{:S(2)}, u32[]{:S(2)}) collective-permute-start(bf16[128,1024]{1,0:T(8,128)(2,1)S(1)} %add_convert_fusion.9), channel_id=1, source_target_pairs={{0,1},{1,2},{2,3},{4,5},{5,6},{6,7},{8,9},{9,10},{10,11},{12,13},{... | collective-permute-start | bytes 786440 | tf_op jit(solution)/shard_map/ppermute | solution.py:398
  309.7 28.0 %collective-permute-start.2 = (bf16[128,1024]{1,0:T(8,128)(2,1)S(1)}, bf16[128,1024]{1,0:T(8,128)(2,1)S(1)}, u32[]{:S(2)}, u32[]{:S(2)}) collective-permute-start(bf16[128,1024]{1,0:T(8,128)(2,1)S(1)} %add_convert_fusion.12), channel_id=1, source_target_pairs={{0,1},{1,2},{2,3},{4,5},{5,6},{6,7},{8,9},{9,10},{10,11},{12,13},{... | collective-permute-start | bytes 786440 | tf_op jit(solution)/shard_map/ppermute | solution.py:398
where the time goes:
time: 355 us; the launch traced here: 351 us
  Pallas kernels  135 us (38%)
  waiting for transfers between devices  108 us (30%)
  starting transfers between devices  71 us (20%)
  other arithmetic  20.8 us (6%)
  local copies, waits for them, and re-layouts  15.9 us (4%)
    all_to_all x6, waiting for transfers between devices, exchange(): got = lax.all_to_all(block, 'dp', split_axis=0, concat_axis=0, tiled=True)  97.7 us
    pallas_call x5, Pallas kernels, layer(): pl.pallas_call(functools.partial(layer_kernel, spans, first_head, heads,...  62.9 us
    ppermute x15, starting transfers between devices, shifted(): return lax.ppermute(block, axis, route)  41.2 us
    pallas_call x5, Pallas kernels, final_state(): pl.pallas_call(functools.partial(state_kernel, spans), grid_spec=pltpu.Pr...  38.9 us
    all_to_all x6, starting transfers between devices, exchange(): got = lax.all_to_all(block, 'dp', split_axis=0, concat_axis=0, tiled=True)  24.6 us
    pallas_call x6, Pallas kernels, collect(): pl.pallas_call(functools.partial(collect_kernel, groups, capacity, column...  23.2 us
    convert_element_type x20, other arithmetic, on_device(): entering = shifted(outgoing.astype(bf16), 'seq', 1).astype(f32)  15.9 us
    ppermute x15, waiting for transfers between devices, shifted(): return lax.ppermute(block, axis, route)  10.1 us
  transfers between devices with their start and end apart: 22, of which 8 were waited for; matrix products, arithmetic and copies ran while one was open for 8% of the time, Pallas kernels for 33%

commit v1 on v0

--- a/solution.py
+++ b/solution.py
@@ -12,7 +12,6 @@
 RUNS = SPAN // SEG
 HALF = SPAN // 2
 LANES = 128
-CHUNK_HEADS = 16
 
 f32, bf16 = jnp.float32, jnp.bfloat16
 ANY = pl.BlockSpec(memory_space=pl.ANY)
@@ -85,7 +84,10 @@
     return send, pick[0]
 
 
-def collect_kernel(groups, capacity, column, width, send_ref, rows_ref, token_ref, out_ref, held, gets, puts):
+def collect_kernel(groups, capacity, parts, send_ref, token_ref, *rest):
+    sources = rest[: len(parts)]
+    out_ref, held, gets, puts = rest[len(parts) :]
+
     def put(group):
         return pltpu.make_async_copy(held.at[group], out_ref.at[group], puts.at[group])
 
@@ -93,11 +95,14 @@
 
         @pl.loop(0, capacity)
         def _(slot):
-            pltpu.make_async_copy(
-                rows_ref.at[send_ref[group, slot], :, pl.ds(column, width)],
-                held.at[group, slot],
-                gets.at[group],
-            ).start()
+            place = 0
+            for source, (column, width) in zip(sources, parts):
+                pltpu.make_async_copy(
+                    source.at[send_ref[group, slot], :, pl.ds(column, width)],
+                    held.at[group, slot, :, pl.ds(place, width)],
+                    gets.at[group],
+                ).start()
+                place += width
 
     for group in range(groups):
         pltpu.make_async_copy(held.at[group], held.at[group], gets.at[group]).wait()
@@ -106,13 +111,14 @@
         put(group).wait()
 
 
-def collect(send, rows, token, groups, capacity, column, width):
+def collect(send, token, sources, parts, groups, capacity):
+    width = sum(part[1] for part in parts)
     return pl.pallas_call(
-        functools.partial(collect_kernel, groups, capacity, column, width),
+        functools.partial(collect_kernel, groups, capacity, parts),
         grid_spec=pltpu.PrefetchScalarGridSpec(
             num_scalar_prefetch=1,
             grid=(1,),
-            in_specs=[ANY, ANY],
+            in_specs=[ANY] * (1 + len(sources)),
             out_specs=ANY,
             scratch_shapes=[
                 pltpu.VMEM((groups, capacity, SEG, width), bf16),
@@ -126,16 +132,18 @@
             flops=0, transcendentals=0, bytes_accessed=4 * groups * capacity * SEG * width
         ),
         name="collect",
-    )(send, rows, token)
-
-
-def fetch_spans(spans, pick_ref, source_ref, held, sems):
+    )(send, token, *sources)
+
+
+def fetch_spans(spans, column, width, pick_ref, source_ref, held, sems):
     @pl.when(pl.program_id(0) == 0)
     def _():
         @pl.loop(0, spans * RUNS)
         def _(run):
             pltpu.make_async_copy(
-                source_ref.at[pick_ref[run]], held.at[run], sems.at[run // RUNS]
+                source_ref.at[pick_ref[run], :, pl.ds(column, width)],
+                held.at[run],
+                sems.at[run // RUNS],
             ).start()
 
 
@@ -148,20 +156,16 @@
 
 def prepare_kernel(
     spans, starts_count, pick_ref, starts_ref, small_ref, decay_ref,
-    cum_ref, bias_ref, entry_ref, end_ref, device_ref, through_ref, keys_ref, query_ref, score_ref,
+    cum_ref, bias_ref, entry_ref, end_ref, through_ref, keys_ref, query_ref, score_ref,
     held, sems, later,
 ):
     step = pl.program_id(0)
     span = spans - 1 - step
 
+    fetch_spans(spans, 0, 3 * LANES, pick_ref, small_ref, held, sems)
+
     @pl.when(step == 0)
     def _():
-        @pl.loop(0, spans * RUNS)
-        def _(run):
-            pltpu.make_async_copy(
-                small_ref.at[pick_ref[run]], held.at[run], sems.at[run // RUNS]
-            ).start()
-
         later[...] = jnp.zeros_like(later)
 
     small = fetched(held, sems, span)
@@ -201,8 +205,6 @@
     entry_ref[...] = split_float(jnp.where(doc == 0, jnp.exp(cum), 0.0))
     at_end = doc == last
     end_ref[...] = split_float(jnp.where(at_end, jnp.exp(to_end), 0.0) * steps)
-    reach = at_end & (after == 0)
-    device_ref[...] = split_float(jnp.where(reach, jnp.exp(to_end + later[...]), 0.0) * steps)
     cum_ref[...] = cum
     bias_ref[...] = (jnp.log(steps) - cum).T
     keys_ref[...] = keys.T.astype(bf16)
@@ -233,7 +235,6 @@
             out_specs=[
                 rows(LANES),
                 pl.BlockSpec((LANES, SPAN), back_lanes),
-                rows(2 * LANES),
                 rows(2 * LANES),
                 rows(2 * LANES),
                 whole((1, LANES)),
@@ -252,7 +253,6 @@
             jax.ShapeDtypeStruct((LANES, tokens), f32),
             jax.ShapeDtypeStruct((tokens, 2 * LANES), bf16),
             jax.ShapeDtypeStruct((tokens, 2 * LANES), bf16),
-            jax.ShapeDtypeStruct((tokens, 2 * LANES), bf16),
             jax.ShapeDtypeStruct((1, LANES), f32),
             jax.ShapeDtypeStruct((LANES, tokens), bf16),
             jax.ShapeDtypeStruct((tokens, LANES), bf16),
@@ -263,59 +263,56 @@
     )(pick, starts, small, decay)
 
 
-def state_kernel(spans, pick_ref, values_ref, keys_ref, device_ref, ones_ref, out_ref, held, sems):
+def correct_kernel(
+    result_ref, entry_ref, query_ref, ones_ref, incoming_ref, out_ref, reach
+):
+    @pl.when(pl.program_id(0) == 0)
+    def _():
+        reach[...] = jnp.ones_like(reach)
+
+    entry = spread(entry_ref[...], ones_ref[...]) * reach[...]
+    from_state = jnp.dot(query_ref[...], incoming_ref[...], preferred_element_type=f32)
+    out_ref[...] = (result_ref[...].astype(f32) + from_state * entry).astype(bf16)
+    reach[...] = entry[SPAN - 1 :, :]
+
+
+def correct(result, entry, query, ones, incoming, column):
+    tokens, full = result.shape
+    width = incoming.shape[-1]
+
+    def rows(lanes, block=0):
+        return pl.BlockSpec((SPAN, lanes), lambda s: (s, block))
+
+    return pl.pallas_call(
+        correct_kernel,
+        grid=(tokens // SPAN,),
+        in_specs=[
+            rows(width, column // width), rows(2 * LANES), rows(LANES),
+            whole((2 * LANES, width)), whole((LANES, width)),
+        ],
+        out_specs=rows(width, column // width),
+        scratch_shapes=[pltpu.VMEM((1, width), f32)],
+        out_shape=jax.ShapeDtypeStruct((tokens, full), bf16),
+        input_output_aliases={0: 0},
+        compiler_params=params(),
+        cost_estimate=pl.CostEstimate(
+            flops=6 * tokens * LANES * width, transcendentals=0, bytes_accessed=4 * tokens * width
+        ),
+        name="correct",
+    )(result, entry, query, ones, incoming)
+
+
+def layer_kernel(
+    spans, first_head, heads, head_width, lead, aliased, pick_ref, values_ref, cum_ref, bias_ref, entry_ref,
+    end_ref, keys_ref, query_ref, score_ref, ones_ref, skip_ref, *rest
+):
+    out_ref, state, held, sems, base = rest[1:] if aliased else rest
     span = pl.program_id(0)
-    fetch_spans(spans, pick_ref, values_ref, held, sems)
+    fetch_spans(spans, lead, heads * head_width, pick_ref, values_ref, held, sems)
 
     @pl.when(span == 0)
     def _():
-        out_ref[...] = jnp.zeros_like(out_ref)
-
-    values = fetched(held, sems, span)
-    scaled = (values * spread(device_ref[...], ones_ref[...])).astype(bf16)
-    out_ref[...] += jnp.dot(keys_ref[...], scaled, preferred_element_type=f32)
-
-
-def final_state(pick, values, keys, device, ones, tokens):
-    spans = tokens // SPAN
-    width = values.shape[-1]
-    return pl.pallas_call(
-        functools.partial(state_kernel, spans),
-        grid_spec=pltpu.PrefetchScalarGridSpec(
-            num_scalar_prefetch=1,
-            grid=(spans,),
-            in_specs=[
-                ANY,
-                pl.BlockSpec((LANES, SPAN), lambda s, *_: (0, s)),
-                pl.BlockSpec((SPAN, 2 * LANES), lambda s, *_: (s, 0)),
-                whole((2 * LANES, width)),
-            ],
-            out_specs=whole((LANES, width)),
-            scratch_shapes=[
-                pltpu.VMEM((tokens // SEG, SEG, width), bf16),
-                pltpu.SemaphoreType.DMA((spans,)),
-            ],
-        ),
-        out_shape=jax.ShapeDtypeStruct((LANES, width), f32),
-        compiler_params=params(),
-        cost_estimate=pl.CostEstimate(
-            flops=6 * tokens * LANES * width, transcendentals=0, bytes_accessed=2 * tokens * width
-        ),
-        name="final_state",
-    )(pick, values, keys, device, ones)
-
-
-def layer_kernel(
-    spans, first_head, heads, head_width, aliased, pick_ref, values_ref, cum_ref, bias_ref, entry_ref,
-    end_ref, keys_ref, query_ref, score_ref, ones_ref, skip_ref, incoming_ref, *rest
-):
-    out_ref, held, sems, state, base = rest[1:] if aliased else rest
-    span = pl.program_id(0)
-    fetch_spans(spans, pick_ref, values_ref, held, sems)
-
-    @pl.when(span == 0)
-    def _():
-        state[...] = incoming_ref[...]
+        state[...] = jnp.zeros_like(state)
 
     values = fetched(held, sems, span)
     ones = ones_ref[...]
@@ -344,10 +341,10 @@
             out_ref[rows, columns] = (base[rows, columns] + total).astype(bf16)
 
 
-def layer(result, pick, values, prepared, ones, skip, incoming, tokens, full, column, first_head, heads):
+def layer(result, pick, values, lead, prepared, ones, skip, tokens, full, column, first_head, heads):
     cum, bias, entry, end, keys, query, scores = prepared
     spans = tokens // SPAN
-    width = values.shape[-1]
+    width = ones.shape[-1]
     aliased = result is not None
 
     def rows(lanes):
@@ -356,32 +353,37 @@
     def lanes():
         return pl.BlockSpec((LANES, SPAN), lambda s, *_: (0, s))
 
-    operands = [pick, values, cum, bias, entry, end, keys, query, scores, ones, skip, incoming]
+    operands = [pick, values, cum, bias, entry, end, keys, query, scores, ones, skip]
     in_specs = [
         ANY, rows(LANES), lanes(), rows(2 * LANES), rows(2 * LANES), lanes(), rows(LANES),
         pl.BlockSpec((1, SPAN, SPAN), lambda s, *_: (s, 0, 0)),
-        whole((2 * LANES, width)), whole((1, width)), whole((LANES, width)),
+        whole((2 * LANES, width)), whole((1, width)),
     ]
     if aliased:
         operands.append(result)
         in_specs.append(ANY)
     return pl.pallas_call(
         functools.partial(
-            layer_kernel, spans, first_head, heads, width // heads, aliased
+            layer_kernel, spans, first_head, heads, width // heads, lead, aliased
         ),
         grid_spec=pltpu.PrefetchScalarGridSpec(
             num_scalar_prefetch=1,
             grid=(spans,),
             in_specs=in_specs,
-            out_specs=pl.BlockSpec((SPAN, width), lambda s, *_: (s, column // width)),
+            out_specs=[
+                pl.BlockSpec((SPAN, width), lambda s, *_: (s, column // width)),
+                whole((LANES, width)),
+            ],
             scratch_shapes=[
                 pltpu.VMEM((tokens // SEG, SEG, width), bf16),
                 pltpu.SemaphoreType.DMA((spans,)),
-                pltpu.VMEM((LANES, width), f32),
                 pltpu.VMEM((SPAN, width), f32),
             ],
         ),
-        out_shape=jax.ShapeDtypeStruct((tokens, full), bf16),
+        out_shape=[
+            jax.ShapeDtypeStruct((tokens, full), bf16),
+            jax.ShapeDtypeStruct((LANES, width), f32),
+        ],
         input_output_aliases={len(operands) - 1: 0} if aliased else {},
         compiler_params=params(),
         cost_estimate=pl.CostEstimate(
@@ -390,6 +392,11 @@
         ),
         name="layer",
     )(*operands)
+
+
+def chunk_plan(heads):
+    unit = heads // 5
+    return (2 * unit, 2 * unit, unit)
 
 
 def shifted(block, axis, distance):
@@ -425,52 +432,55 @@
         got = lax.all_to_all(block, "dp", split_axis=0, concat_axis=0, tiled=True)
         return got.reshape(groups * capacity, SEG, block.shape[-1])
 
-    small_sent = collect(send, small, send, groups, capacity, 0, 3 * LANES)
-    small_got = exchange(small_sent)
-
-    chunk = CHUNK_HEADS
-    count = heads // chunk
-    width = chunk * head_width
-    sent = []
-    got = []
-    for number in range(count):
+    plan = chunk_plan(heads)
+    blocks = []
+    first = 0
+    for count in plan:
+        blocks.append((first, count, first * head_width, count * head_width))
+        first += count
+    lead = 3 * LANES
+
+    def gathered(number, token):
+        _, _, column, width = blocks[number]
         if number == 0:
-            token = small_sent
-        elif number == 1:
-            token = sent[0]
-        else:
-            token = got[number - 2]
-        block = collect(send, values, token, groups, capacity, number * width, width)
-        sent.append(block)
-        got.append(exchange(block))
-
+            parts = ((0, lead), (column, width))
+            return collect(send, token, (small, values), parts, groups, capacity)
+        return collect(send, token, (values,), ((column, width),), groups, capacity)
+
+    lane_head = jnp.arange(full) // head_width
+    ones = (jnp.arange(2 * LANES)[:, None] % LANES == lane_head[None, :]).astype(bf16)
+    skip = jnp.repeat(skip_gain, head_width)[None, :]
     starts = document_starts[0] - lax.axis_index("seq").astype(jnp.int32) * tokens
     decay = jnp.pad(decay_log, (0, pad))[None, :]
-    prepared = prepare(pick, starts, small_got, decay, tokens)
-    cum, bias, entry, end, device, through, keys, query, scores = prepared
-    lane_head = jnp.arange(full) // head_width
-    ones = (jnp.arange(2 * LANES)[:, None] % LANES == lane_head[None, :]).astype(bf16)
-    through = jnp.repeat(through[0, :heads], head_width)[None, :]
-    skip = jnp.repeat(skip_gain, head_width)[None, :]
-
-    incoming = []
-    for number in range(count):
-        part = slice(number * width, (number + 1) * width)
-        final = final_state(pick, got[number], keys, device, ones[:, part], tokens)
-        entering = jnp.zeros_like(final)
-        for hop in range(shards - 1):
-            outgoing = through[:, part] * entering + final
-            entering = shifted(outgoing.astype(bf16), "seq", 1).astype(f32)
-        incoming.append(entering)
-
+
+    sent = [gathered(0, send)]
+    sent.append(gathered(1, sent[0]))
     result = None
-    for number in range(count):
-        part = slice(number * width, (number + 1) * width)
-        result = layer(
-            result, pick, got[number], (cum, bias, entry, end, keys, query, scores),
-            ones[:, part], skip[:, part], incoming[number], tokens, full, number * width,
-            number * chunk, chunk,
+    finals = []
+    for number in range(len(blocks)):
+        first_head, count, column, width = blocks[number]
+        got = exchange(sent[number])
+        if number == 0:
+            prepared = prepare(pick, starts, got, decay, tokens)
+            cum, bias, entry, end, through, keys, query, scores = prepared
+            through = jnp.repeat(through[0, :heads], head_width)[None, :]
+        part = slice(column, column + width)
+        result, final = layer(
+            result, pick, got, lead if number == 0 else 0,
+            (cum, bias, entry, end, keys, query, scores),
+            ones[:, part], skip[:, part], tokens, full, column, first_head, count,
         )
+        finals.append(final)
+        if number + 2 < len(blocks):
+            sent.append(gathered(number + 2, final))
+
+    for (first_head, count, column, width), final in zip(blocks, finals):
+        part = slice(column, column + width)
+        entering = shifted(final.astype(bf16), "seq", 1)
+        for hop in range(shards - 2):
+            outgoing = through[:, part] * entering.astype(f32) + final
+            entering = shifted(outgoing.astype(bf16), "seq", 1)
+        result = correct(result, entry, query, ones[:, part], entering, column)
     return result[None]
 
 

time: 355 us -> 295 us (0.83)
  Pallas kernels: 135 us -> 104 us
  starting transfers between devices: 71 us -> 52.2 us
  other arithmetic: 20.8 us -> 8.49 us
  waiting for transfers between devices: 108 us -> 113 us
    pallas_call x11 -> x6, Pallas kernels: 62.1 us -> 40.5 us  [the longest x3 24.2 us: correct(): pl.pallas_call(correct_kernel, grid=(tokens // SPAN,), in_specs=[rows(wid...]
    convert_element_type x20 -> x9, other arithmetic: 15.9 us -> 5.12 us  [the longest x3 2.58 us: on_device(): entering = shifted(final.astype(bf16), 'seq', 1)]
    all_to_all x6 -> x3, starting transfers between devices: 24.6 us -> 13.9 us  [exchange(): got = lax.all_to_all(block, 'dp', split_axis=0, concat_axis=0, tiled=True)]
    ppermute x15 -> x9, waiting for transfers between devices: 10.1 us -> 19.7 us  [shifted(): return lax.ppermute(block, axis, route)]
    pallas_call x5 -> x3, Pallas kernels: 62.9 us -> 54.2 us  [layer(): pl.pallas_call(functools.partial(layer_kernel, spans, first_head, heads,...]
    ppermute x15 -> x9, starting transfers between devices: 41.2 us -> 33.2 us  [shifted(): return lax.ppermute(block, axis, route)]
    all_to_all x6 -> x3, waiting for transfers between devices: 97.7 us -> 93.5 us  [exchange(): got = lax.all_to_all(block, 'dp', split_axis=0, concat_axis=0, tiled=True)]
    unnamed x29 -> x25, local copies, waits for them, and re-layouts: 8.58 us -> 6.73 us
  transfers between devices with their start and end apart: 22 -> 13, of which waited for: 8 -> 5; matrix products, arithmetic and copies ran while one was open for 8% -> 6% of each run, Pallas kernels for 33% -> 31%
where the time goes in v1:
time: 295 us; the launch traced here: 293 us
  waiting for transfers between devices  113 us (38%)
  Pallas kernels  104 us (35%)
  starting transfers between devices  52.2 us (18%)
  local copies, waits for them, and re-layouts  14.3 us (5%)
  other arithmetic  8.49 us (3%)
    all_to_all x3, waiting for transfers between devices, exchange(): got = lax.all_to_all(block, 'dp', split_axis=0, concat_axis=0, tiled=True)  93.5 us
    pallas_call x3, Pallas kernels, layer(): pl.pallas_call(functools.partial(layer_kernel, spans, first_head, heads,...  54.2 us
    ppermute x9, starting transfers between devices, shifted(): return lax.ppermute(block, axis, route)  33.2 us
    pallas_call x3, Pallas kernels, correct(): pl.pallas_call(correct_kernel, grid=(tokens // SPAN,), in_specs=[rows(wid...  24.2 us
    ppermute x9, waiting for transfers between devices, shifted(): return lax.ppermute(block, axis, route)  19.7 us
    pallas_call x3, Pallas kernels, collect(): pl.pallas_call(functools.partial(collect_kernel, groups, capacity, parts)...  16.3 us
    all_to_all x3, starting transfers between devices, exchange(): got = lax.all_to_all(block, 'dp', split_axis=0, concat_axis=0, tiled=True)  13.9 us
    pallas_call x1, Pallas kernels, prepare(): pl.pallas_call(functools.partial(prepare_kernel, spans, starts_count), gr...  8.04 us
  transfers between devices with their start and end apart: 13, of which 5 were waited for; matrix products, arithmetic and copies ran while one was open for 6% of the time, Pallas kernels for 31%

profile of v1, /device:TPU:0, one launch (start us, length us, event | category | flops | bytes accessed | tf_op | source)
XLA Modules:
  0.0 292.8 jit_solution(1714902631062280177)
XLA Ops:
  0.0 0.7 reduce
  0.9 0.6 broadcast_in_dim.23
  1.6 5.2 %all-to-all-start = ((s32[8,1,160]{2,1,0:T(1,128)}), s32[8,1,160]{2,1,0:T(1,128)S(1)}, u32[]{:S(2)}, u32[]{:S(2)}) async-start(s32[8,1,160]{2,1,0:T(1,128)} %broadcast_in_dim.23), calls=%async_computation | async-start | bytes 16384 | tf_op jit(solution)/shard_map/all_to_all | solution.py:421
  6.8 1.1 copy.20
  7.9 1.1 copy.21
  9.0 1.0 fusion.1
  10.6 1.3 copy.22
  11.9 0.6 copy.25
  12.5 1.6 plan.1
  14.1 6.8 %collect.3.token_ref = bf16[8,21,8,2432]{3,2,1,0:T(8,128)(2,1)} custom-call(s32[8,128]{1,0:T(8,128)} %get-tuple-element.22.send_ref.token_ref, s32[8,128]{1,0:T(8,128)} %get-tuple-element.22.send_ref.token_ref, bf16[160,8,384]{2,1,0:T(8,128)(2,1)} %bitcast.24, bf16[160,8,5120]{2,1,0:T(8,128)(2,1)} %bitcast.21), custom_call_target="tpu_custom_call" | custom-call | bytes 13074432 | tf_op jit(solution)/shard_map/collect/pallas_call | solution.py:116
  21.0 4.8 %all-to-all-start.1 = ((bf16[8,21,8,2432]{3,2,1,0:T(8,128)(2,1)}), bf16[8,21,8,2432]{3,2,1,0:T(8,128)(2,1)}, u32[]{:S(2)}, u32[]{:S(2)}) async-start(bf16[8,21,8,2432]{3,2,1,0:T(8,128)(2,1)} %collect.3.token_ref), calls=%async_computation.1 | async-start | bytes 13074432 | tf_op jit(solution)/shard_map/all_to_all | solution.py:432
  25.8 5.6 %collect.5 = bf16[8,21,8,2048]{3,2,1,0:T(8,128)(2,1)} custom-call(s32[8,128]{1,0:T(8,128)} %get-tuple-element.22.send_ref.token_ref, bf16[8,21,8,2432]{3,2,1,0:T(8,128)(2,1)} %collect.3.token_ref, bf16[160,8,5120]{2,1,0:T(8,128)(2,1)} %bitcast.22), custom_call_target="tpu_custom_call" | custom-call | bytes 11010048 | tf_op jit(solution)/shard_map/collect/pallas_call | solution.py:116
  31.4 68.6 %all-to-all-done.1 = bf16[8,21,8,2432]{3,2,1,0:T(8,128)(2,1)} async-done(((bf16[8,21,8,2432]{3,2,1,0:T(8,128)(2,1)}), bf16[8,21,8,2432]{3,2,1,0:T(8,128)(2,1)}, u32[]{:S(2)}, u32[]{:S(2)}) %all-to-all-start.1) | async-done | bytes 6537248 | tf_op jit(solution)/shard_map/all_to_all | solution.py:432
  100.0 4.7 %all-to-all-start.3 = ((bf16[8,21,8,2048]{3,2,1,0:T(8,128)(2,1)}), bf16[8,21,8,2048]{3,2,1,0:T(8,128)(2,1)}, u32[]{:S(2)}, u32[]{:S(2)}) async-start(bf16[8,21,8,2048]{3,2,1,0:T(8,128)(2,1)} %collect.5), calls=%async_computation.3 | async-start | bytes 11010048 | tf_op jit(solution)/shard_map/all_to_all | solution.py:432
  105.8 0.6 fusion.7
  107.0 1.5 copy-done.1
  108.5 1.5 fusion.5
  110.0 8.0 %prepare.1 = (f32[1280,128]{1,0:T(8,128)}, f32[128,1280]{1,0:T(8,128)}, bf16[1280,256]{1,0:T(8,128)(2,1)}, bf16[1280,256]{1,0:T(8,128)(2,1)}, f32[1,128]{1,0:T(1...) custom-call(s32[160]{0:T(256)} %bitcast.32, ...), custom_call_target="tpu_custom_call" | custom-call | tf_op jit(solution)/shard_map/prepare/pallas_call | solution.py:229
  118.0 20.9 %layer.3 = (bf16[1280,5120]{1,0:T(8,128)(2,1)}, f32[128,2048]{1,0:T(8,128)}) custom-call(s32[160]{0:T(256)} %bitcast.33, bf16[168,8,2432]{2,1,0:T(8,128)(2,1)} %bitcast.4.small_ref.values_ref, f32[1280,128]{1,0:T(8,128)} %get-tuple-element.23.cum_ref, f32[128,1280]{1,0:T(8,128)} %get-tuple-element.24.bias_ref, ...), custom_call_target="tpu_custom_call" | custom-call | flops 5368709120 | bytes 10485760 | tf_op jit(solution)/shard_map/layer/pallas_call | solution.py:365
  138.9 3.9 %collect.4 = bf16[8,21,8,1024]{3,2,1,0:T(8,128)(2,1)} custom-call(s32[8,128]{1,0:T(8,128)} %get-tuple-element.22.send_ref.token_ref, f32[128,2048]{1,0:T(8,128)} %get-tuple-element.30.token_ref, bf16[160,8,5120]{2,1,0:T(8,128)(2,1)} %bitcast.23), custom_call_target="tpu_custom_call" | custom-call | bytes 5505024 | tf_op jit(solution)/shard_map/collect/pallas_call | solution.py:116
  142.8 24.9 %all-to-all-done.3 = bf16[8,21,8,2048]{3,2,1,0:T(8,128)(2,1)} async-done(((bf16[8,21,8,2048]{3,2,1,0:T(8,128)(2,1)}), bf16[8,21,8,2048]{3,2,1,0:T(8,128)(2,1)}, u32[]{:S(2)}, u32[]{:S(2)}) %all-to-all-start.3) | async-done | bytes 5505056 | tf_op jit(solution)/shard_map/all_to_all | solution.py:432
  167.8 4.4 %all-to-all-start.2 = ((bf16[8,21,8,1024]{3,2,1,0:T(8,128)(2,1)}), bf16[8,21,8,1024]{3,2,1,0:T(8,128)(2,1)}, u32[]{:S(2)}, u32[]{:S(2)}) async-start(bf16[8,21,8,1024]{3,2,1,0:T(8,128)(2,1)} %collect.4), calls=%async_computation.2 | async-start | bytes 5505024 | tf_op jit(solution)/shard_map/all_to_all | solution.py:432
  172.2 0.6 slice.60.skip_ref
  172.8 1.9 slice.59.ones_ref
  174.7 3.5 %collective-permute-start = (bf16[128,2048]{1,0:T(8,128)(2,1)S(1)}, bf16[128,2048]{1,0:T(8,128)(2,1)S(1)}, u32[]{:S(2)}, u32[]{:S(2)}) collective-permute-start(bf16[128,2048]{1,0:T(8,128)(2,1)S(1)} %convert_element_type.63), channel_id=1, source_target_pairs={{0,1},{1,2},{2,3},{4,5},{5,6},{6,7},{8,9},{9,10},{10,11},{12,13},{... | collective-permute-start | bytes 1572872 | tf_op jit(solution)/shard_map/ppermute | solution.py:405
  178.2 20.9 %layer.4 = (bf16[1280,5120]{1,0:T(8,128)(2,1)}, f32[128,2048]{1,0:T(8,128)}) custom-call(s32[160]{0:T(256)} %bitcast.34, bf16[168,8,2048]{2,1,0:T(8,128)(2,1)} %bitcast.8.values_ref, f32[1280,128]{1,0:T(8,128)} %get-tuple-element.23.cum_ref, f32[128,1280]{1,0:T(8,128)} %get-tuple-element.24.bias_ref, ...), custom_call_target="tpu_custom_call", output_to_operand_aliasing={{0}: (11, {})} | custom-call | flops 5368709120 | bytes 10485760 | tf_op jit(solution)/shard_map/layer/pallas_call | solution.py:365
  199.3 1.4 convert_element_type.68
  200.7 3.5 %collective-permute-start.3 = (bf16[128,2048]{1,0:T(8,128)(2,1)S(1)}, bf16[128,2048]{1,0:T(8,128)(2,1)S(1)}, u32[]{:S(2)}, u32[]{:S(2)}) collective-permute-start(bf16[128,2048]{1,0:T(8,128)(2,1)S(1)} %convert_element_type.68), channel_id=1, source_target_pairs={{0,1},{1,2},{2,3},{4,5},{5,6},{6,7},{8,9},{9,10},{10,11},{12,13},{... | collective-permute-start | bytes 1572872 | tf_op jit(solution)/shard_map/ppermute | solution.py:405
  204.3 0.9 add_convert_fusion.3
  205.2 4.2 %collective-permute-start.1 = (bf16[128,2048]{1,0:T(8,128)(2,1)}, bf16[128,2048]{1,0:T(8,128)(2,1)}, u32[]{:S(2)}, u32[]{:S(2)}) collective-permute-start(bf16[128,2048]{1,0:T(8,128)(2,1)} %add_convert_fusion.3), channel_id=1, source_target_pairs={{0,1},{1,2},{2,3},{4,5},{5,6},{6,7},{8,9},{9,10},{10,11},{12,13},{... | collective-permute-start | bytes 1572872 | tf_op jit(solution)/shard_map/ppermute | solution.py:405
  209.5 7.0 %collective-permute-done.3 = bf16[128,2048]{1,0:T(8,128)(2,1)S(1)} collective-permute-done((bf16[128,2048]{1,0:T(8,128)(2,1)S(1)}, bf16[128,2048]{1,0:T(8,128)(2,1)S(1)}, u32[]{:S(2)}, u32[]{:S(2)}) %collective-permute-start.3) | collective-permute-done | bytes 524320 | tf_op jit(solution)/shard_map/ppermute | solution.py:405
  216.7 4.6 %collective-permute-start.4 = (bf16[128,2048]{1,0:T(8,128)(2,1)S(1)}, bf16[128,2048]{1,0:T(8,128)(2,1)S(1)}, u32[]{:S(2)}, u32[]{:S(2)}) collective-permute-start(bf16[128,2048]{1,0:T(8,128)(2,1)S(1)} %add_convert_fusion.1), channel_id=1, source_target_pairs={{0,1},{1,2},{2,3},{4,5},{5,6},{6,7},{8,9},{9,10},{10,11},{12,13},{... | collective-permute-start | bytes 1572872 | tf_op jit(solution)/shard_map/ppermute | solution.py:405
  221.3 12.4 %layer.5 = (bf16[1280,5120]{1,0:T(8,128)(2,1)}, f32[128,1024]{1,0:T(8,128)}) custom-call(s32[160]{0:T(256)} %bitcast.35, bf16[168,8,1024]{2,1,0:T(8,128)(2,1)} %bitcast.7.values_ref, f32[1280,128]{1,0:T(8,128)} %get-tuple-element.23.cum_ref, f32[128,1280]{1,0:T(8,128)} %get-tuple-element.24.bias_ref, ...), custom_call_target="tpu_custom_call", output_to_operand_aliasing={{0}: (11, {})} | custom-call | flops 2684354560 | bytes 5242880 | tf_op jit(solution)/shard_map/layer/pallas_call | solution.py:365
  233.7 1.1 convert_element_type.73
  234.8 3.5 %collective-permute-start.6 = (bf16[128,1024]{1,0:T(8,128)(2,1)S(1)}, bf16[128,1024]{1,0:T(8,128)(2,1)S(1)}, u32[]{:S(2)}, u32[]{:S(2)}) collective-permute-start(bf16[128,1024]{1,0:T(8,128)(2,1)S(1)} %convert_element_type.73), channel_id=1, source_target_pairs={{0,1},{1,2},{2,3},{4,5},{5,6},{6,7},{8,9},{9,10},{10,11},{12,13},{... | collective-permute-start | bytes 786440 | tf_op jit(solution)/shard_map/ppermute | solution.py:405
  238.3 1.2 add_convert_fusion.2
  239.5 1.9 collective-permute-start.2
  241.5 3.5 %collective-permute-done.6 = bf16[128,1024]{1,0:T(8,128)(2,1)S(1)} collective-permute-done((bf16[128,1024]{1,0:T(8,128)(2,1)S(1)}, bf16[128,1024]{1,0:T(8,128)(2,1)S(1)}, u32[]{:S(2)}, u32[]{:S(2)}) %collective-permute-start.6) | collective-permute-done | bytes 262176 | tf_op jit(solution)/shard_map/ppermute | solution.py:405
  245.1 4.4 %collective-permute-start.7 = (bf16[128,1024]{1,0:T(8,128)(2,1)S(1)}, bf16[128,1024]{1,0:T(8,128)(2,1)S(1)}, u32[]{:S(2)}, u32[]{:S(2)}) collective-permute-start(bf16[128,1024]{1,0:T(8,128)(2,1)S(1)} %add_convert_fusion.5), channel_id=1, source_target_pairs={{0,1},{1,2},{2,3},{4,5},{5,6},{6,7},{8,9},{9,10},{10,11},{12,13},{... | collective-permute-start | bytes 786440 | tf_op jit(solution)/shard_map/ppermute | solution.py:405
  249.6 3.1 %collective-permute-start.5 = (bf16[128,2048]{1,0:T(8,128)(2,1)S(1)}, bf16[128,2048]{1,0:T(8,128)(2,1)S(1)}, u32[]{:S(2)}, u32[]{:S(2)}) collective-permute-start(bf16[128,2048]{1,0:T(8,128)(2,1)S(1)} %add_convert_fusion), channel_id=1, source_target_pairs={{0,1},{1,2},{2,3},{4,5},{5,6},{6,7},{8,9},{9,10},{10,11},{12,13},{... | collective-permute-start | bytes 1572872 | tf_op jit(solution)/shard_map/ppermute | solution.py:405
  252.8 9.1 %collective-permute-done.7 = bf16[128,1024]{1,0:T(8,128)(2,1)S(1)} collective-permute-done((bf16[128,1024]{1,0:T(8,128)(2,1)S(1)}, bf16[128,1024]{1,0:T(8,128)(2,1)S(1)}, u32[]{:S(2)}, u32[]{:S(2)}) %collective-permute-start.7) | collective-permute-done | bytes 262176 | tf_op jit(solution)/shard_map/ppermute | solution.py:405
  261.9 4.4 %collective-permute-start.8 = (bf16[128,1024]{1,0:T(8,128)(2,1)S(1)}, bf16[128,1024]{1,0:T(8,128)(2,1)S(1)}, u32[]{:S(2)}, u32[]{:S(2)}) collective-permute-start(bf16[128,1024]{1,0:T(8,128)(2,1)S(1)} %add_convert_fusion.4), channel_id=1, source_target_pairs={{0,1},{1,2},{2,3},{4,5},{5,6},{6,7},{8,9},{9,10},{10,11},{12,13},{... | collective-permute-start | bytes 786440 | tf_op jit(solution)/shard_map/ppermute | solution.py:405
  266.3 0.8 copy-done.4
  267.1 8.9 %correct.3.result_ref = bf16[1280,5120]{1,0:T(8,128)(2,1)} custom-call(bf16[1280,5120]{1,0:T(8,128)(2,1)} %get-tuple-element.33.result_ref, bf16[1280,256]{1,0:T(8,128)(2,1)} %get-tuple-element.25.entry_ref, bf16[1280,128]{1,0:T(8,128)(2,1)} %get-tuple-element.28.query_ref, ...), custom_call_target="tpu_custom_call", output_to_operand_aliasing={{}: (0, {})} | custom-call | flops 2013265920 | bytes 10485760 | tf_op jit(solution)/shard_map/correct/pallas_call | solution.py:286
  276.0 0.8 copy-done.5
  276.8 8.9 %correct.4.result_ref = bf16[1280,5120]{1,0:T(8,128)(2,1)} custom-call(bf16[1280,5120]{1,0:T(8,128)(2,1)} %correct.3.result_ref, bf16[1280,256]{1,0:T(8,128)(2,1)} %get-tuple-element.25.entry_ref, bf16[1280,128]{1,0:T(8,128)(2,1)} %get-tuple-element.28.query_ref, bf16[256,2048]{1,0:T(8,128)(2,1)} %get-tuple-element.37.ones_ref, ...), custom_call_target="tpu_custom_call", output_to_operand_aliasing={{}: (0, {})} | custom-call | flops 2013265920 | bytes 10485760 | tf_op jit(solution)/shard_map/correct/pallas_call | solution.py:286
  285.7 0.7 copy-done.6
  286.4 6.4 %correct.5 = bf16[1280,5120]{1,0:T(8,128)(2,1)} custom-call(bf16[1280,5120]{1,0:T(8,128)(2,1)} %correct.4.result_ref, bf16[1280,256]{1,0:T(8,128)(2,1)} %get-tuple-element.25.entry_ref, bf16[1280,128]{1,0:T(8,128)(2,1)} %get-tuple-element.28.query_ref, bf16[256,1024]{1,0:T(8,128)(2,1)} %slice.59.ones_ref, ...), custom_call_target="tpu_custom_call", output_to_operand_aliasing={{}: (0, {})} | custom-call | flops 1006632960 | bytes 5242880 | tf_op jit(solution)/shard_map/correct/pallas_call | solution.py:286
  (47 shorter events, 3.2 us)
Async XLA Ops:
  1.6 10.4 %all-to-all-start = ((s32[8,1,160]{2,1,0:T(1,128)}), s32[8,1,160]{2,1,0:T(1,128)S(1)}, u32[]{:S(2)}, u32[]{:S(2)}) async-start(s32[8,1,160]{2,1,0:T(1,128)} %broadcast_in_dim.23), calls=%async_computation | async-start | bytes 16384 | tf_op jit(solution)/shard_map/all_to_all | solution.py:421
  21.0 79.0 %all-to-all-start.1 = ((bf16[8,21,8,2432]{3,2,1,0:T(8,128)(2,1)}), bf16[8,21,8,2432]{3,2,1,0:T(8,128)(2,1)}, u32[]{:S(2)}, u32[]{:S(2)}) async-start(bf16[8,21,8,2432]{3,2,1,0:T(8,128)(2,1)} %collect.3.token_ref), calls=%async_computation.1 | async-start | bytes 13074432 | tf_op jit(solution)/shard_map/all_to_all | solution.py:432
  31.3 73.3 %copy-start.7 = (f32[80]{0:T(128)S(1)}, f32[80]{0:T(128)}, u32[]{:S(2)}) copy-start(f32[80]{0:T(128)} %param.13) | copy-start | bytes 964
  31.4 73.5 %copy-start.8 = (f32[80]{0:T(128)S(1)}, f32[80]{0:T(128)}, u32[]{:S(2)}) copy-start(f32[80]{0:T(128)} %param.12) | copy-start | bytes 964
  31.4 74.0 %copy-start.9 = (s32[1,6]{1,0:T(1,128)S(1)}, s32[1,6]{1,0:T(1,128)}, u32[]{:S(2)}) copy-start(s32[1,6]{1,0:T(1,128)} %param.15) | copy-start | bytes 76
  100.0 67.8 %all-to-all-start.3 = ((bf16[8,21,8,2048]{3,2,1,0:T(8,128)(2,1)}), bf16[8,21,8,2048]{3,2,1,0:T(8,128)(2,1)}, u32[]{:S(2)}, u32[]{:S(2)}) async-start(bf16[8,21,8,2048]{3,2,1,0:T(8,128)(2,1)} %collect.5), calls=%async_computation.3 | async-start | bytes 11010048 | tf_op jit(solution)/shard_map/all_to_all | solution.py:432
  107.0 1.5 copy-start.1
  142.8 31.8 %copy-start = (f32[128,2048]{1,0:T(8,128)S(1)}, f32[128,2048]{1,0:T(8,128)}, u32[]{:S(2)}) copy-start(f32[128,2048]{1,0:T(8,128)} %get-tuple-element.30.token_ref) | copy-start | bytes 3145732
  167.8 53.5 %all-to-all-start.2 = ((bf16[8,21,8,1024]{3,2,1,0:T(8,128)(2,1)}), bf16[8,21,8,1024]{3,2,1,0:T(8,128)(2,1)}, u32[]{:S(2)}, u32[]{:S(2)}) async-start(bf16[8,21,8,1024]{3,2,1,0:T(8,128)(2,1)} %collect.4), calls=%async_computation.2 | async-start | bytes 5505024 | tf_op jit(solution)/shard_map/all_to_all | solution.py:432
  174.7 29.5 %collective-permute-start = (bf16[128,2048]{1,0:T(8,128)(2,1)S(1)}, bf16[128,2048]{1,0:T(8,128)(2,1)S(1)}, u32[]{:S(2)}, u32[]{:S(2)}) collective-permute-start(bf16[128,2048]{1,0:T(8,128)(2,1)S(1)} %convert_element_type.63), channel_id=1, source_target_pairs={{0,1},{1,2},{2,3},{4,5},{5,6},{6,7},{8,9},{9,10},{10,11},{12,13},{... | collective-permute-start | bytes 1572872 | tf_op jit(solution)/shard_map/ppermute | solution.py:405
  178.2 20.9 %copy-start.10 = (f32[1,128]{1,0:T(1,128)S(1)}, f32[1,128]{1,0:T(1,128)}, u32[]{:S(2)}) copy-start(f32[1,128]{1,0:T(1,128)} %get-tuple-element.34) | copy-start | bytes 1540
  199.1 17.4 %copy-start.2 = (f32[128,2048]{1,0:T(8,128)S(1)}, f32[128,2048]{1,0:T(8,128)}, u32[]{:S(2)}) copy-start(f32[128,2048]{1,0:T(8,128)} %get-tuple-element.35) | copy-start | bytes 3145732
  200.7 15.8 %collective-permute-start.3 = (bf16[128,2048]{1,0:T(8,128)(2,1)S(1)}, bf16[128,2048]{1,0:T(8,128)(2,1)S(1)}, u32[]{:S(2)}, u32[]{:S(2)}) collective-permute-start(bf16[128,2048]{1,0:T(8,128)(2,1)S(1)} %convert_element_type.68), channel_id=1, source_target_pairs={{0,1},{1,2},{2,3},{4,5},{5,6},{6,7},{8,9},{9,10},{10,11},{12,13},{... | collective-permute-start | bytes 1572872 | tf_op jit(solution)/shard_map/ppermute | solution.py:405
  205.2 33.1 %collective-permute-start.1 = (bf16[128,2048]{1,0:T(8,128)(2,1)}, bf16[128,2048]{1,0:T(8,128)(2,1)}, u32[]{:S(2)}, u32[]{:S(2)}) collective-permute-start(bf16[128,2048]{1,0:T(8,128)(2,1)} %add_convert_fusion.3), channel_id=1, source_target_pairs={{0,1},{1,2},{2,3},{4,5},{5,6},{6,7},{8,9},{9,10},{10,11},{12,13},{... | collective-permute-start | bytes 1572872 | tf_op jit(solution)/shard_map/ppermute | solution.py:405
  216.7 32.8 %collective-permute-start.4 = (bf16[128,2048]{1,0:T(8,128)(2,1)S(1)}, bf16[128,2048]{1,0:T(8,128)(2,1)S(1)}, u32[]{:S(2)}, u32[]{:S(2)}) collective-permute-start(bf16[128,2048]{1,0:T(8,128)(2,1)S(1)} %add_convert_fusion.1), channel_id=1, source_target_pairs={{0,1},{1,2},{2,3},{4,5},{5,6},{6,7},{8,9},{9,10},{10,11},{12,13},{... | collective-permute-start | bytes 1572872 | tf_op jit(solution)/shard_map/ppermute | solution.py:405
  233.7 11.3 %copy-start.3 = (f32[128,1024]{1,0:T(8,128)S(1)}, f32[128,1024]{1,0:T(8,128)}, u32[]{:S(2)}) copy-start(f32[128,1024]{1,0:T(8,128)} %get-tuple-element.36) | copy-start | bytes 1572868
  234.8 10.1 %collective-permute-start.6 = (bf16[128,1024]{1,0:T(8,128)(2,1)S(1)}, bf16[128,1024]{1,0:T(8,128)(2,1)S(1)}, u32[]{:S(2)}, u32[]{:S(2)}) collective-permute-start(bf16[128,1024]{1,0:T(8,128)(2,1)S(1)} %convert_element_type.73), channel_id=1, source_target_pairs={{0,1},{1,2},{2,3},{4,5},{5,6},{6,7},{8,9},{9,10},{10,11},{12,13},{... | collective-permute-start | bytes 786440 | tf_op jit(solution)/shard_map/ppermute | solution.py:405
  239.5 26.8 %collective-permute-start.2 = (bf16[128,2048]{1,0:T(8,128)(2,1)S(1)}, bf16[128,2048]{1,0:T(8,128)(2,1)S(1)}, u32[]{:S(2)}, u32[]{:S(2)}) collective-permute-start(bf16[128,2048]{1,0:T(8,128)(2,1)S(1)} %add_convert_fusion.2), channel_id=1, source_target_pairs={{0,1},{1,2},{2,3},{4,5},{5,6},{6,7},{8,9},{9,10},{10,11},{12,13},{... | collective-permute-start | bytes 1572872 | tf_op jit(solution)/shard_map/ppermute | solution.py:405
  245.1 16.8 %collective-permute-start.7 = (bf16[128,1024]{1,0:T(8,128)(2,1)S(1)}, bf16[128,1024]{1,0:T(8,128)(2,1)S(1)}, u32[]{:S(2)}, u32[]{:S(2)}) collective-permute-start(bf16[128,1024]{1,0:T(8,128)(2,1)S(1)} %add_convert_fusion.5), channel_id=1, source_target_pairs={{0,1},{1,2},{2,3},{4,5},{5,6},{6,7},{8,9},{9,10},{10,11},{12,13},{... | collective-permute-start | bytes 786440 | tf_op jit(solution)/shard_map/ppermute | solution.py:405
  249.6 26.4 %collective-permute-start.5 = (bf16[128,2048]{1,0:T(8,128)(2,1)S(1)}, bf16[128,2048]{1,0:T(8,128)(2,1)S(1)}, u32[]{:S(2)}, u32[]{:S(2)}) collective-permute-start(bf16[128,2048]{1,0:T(8,128)(2,1)S(1)} %add_convert_fusion), channel_id=1, source_target_pairs={{0,1},{1,2},{2,3},{4,5},{5,6},{6,7},{8,9},{9,10},{10,11},{12,13},{... | collective-permute-start | bytes 1572872 | tf_op jit(solution)/shard_map/ppermute | solution.py:405
  261.9 23.8 %collective-permute-start.8 = (bf16[128,1024]{1,0:T(8,128)(2,1)S(1)}, bf16[128,1024]{1,0:T(8,128)(2,1)S(1)}, u32[]{:S(2)}, u32[]{:S(2)}) collective-permute-start(bf16[128,1024]{1,0:T(8,128)(2,1)S(1)} %add_convert_fusion.4), channel_id=1, source_target_pairs={{0,1},{1,2},{2,3},{4,5},{5,6},{6,7},{8,9},{9,10},{10,11},{12,13},{... | collective-permute-start | bytes 786440 | tf_op jit(solution)/shard_map/ppermute | solution.py:405
  266.3 0.8 copy-start.4
  276.0 0.8 copy-start.5
  285.7 0.7 copy-start.6

commit v2 on v1

--- a/solution.py
+++ b/solution.py
@@ -395,8 +395,8 @@
 
 
 def chunk_plan(heads):
-    unit = heads // 5
-    return (2 * unit, 2 * unit, unit)
+    unit = heads // 10
+    return ((4 * unit, 4 * unit), (0, 3 * unit), (8 * unit, 2 * unit), (3 * unit, unit))
 
 
 def shifted(block, axis, distance):
@@ -432,12 +432,9 @@
         got = lax.all_to_all(block, "dp", split_axis=0, concat_axis=0, tiled=True)
         return got.reshape(groups * capacity, SEG, block.shape[-1])
 
-    plan = chunk_plan(heads)
-    blocks = []
-    first = 0
-    for count in plan:
-        blocks.append((first, count, first * head_width, count * head_width))
-        first += count
+    blocks = [
+        (first, count, first * head_width, count * head_width) for first, count in chunk_plan(heads)
+    ]
     lead = 3 * LANES
 
     def gathered(number, token):
@@ -453,10 +450,26 @@
     starts = document_starts[0] - lax.axis_index("seq").astype(jnp.int32) * tokens
     decay = jnp.pad(decay_log, (0, pad))[None, :]
 
+    def entering_state(number, final):
+        _, _, column, width = blocks[number]
+        part = slice(column, column + width)
+        entering = shifted(final.astype(bf16), "seq", 1)
+        for hop in range(shards - 2):
+            outgoing = through[:, part] * entering.astype(f32) + final
+            entering = shifted(outgoing.astype(bf16), "seq", 1)
+        return entering
+
+    def corrected(result, number):
+        _, _, column, width = blocks[number]
+        return correct(
+            result, entry, query, ones[:, column : column + width], incoming[number], column
+        )
+
     sent = [gathered(0, send)]
     sent.append(gathered(1, sent[0]))
     result = None
-    finals = []
+    incoming = []
+    waiting = []
     for number in range(len(blocks)):
         first_head, count, column, width = blocks[number]
         got = exchange(sent[number])
@@ -470,17 +483,13 @@
             (cum, bias, entry, end, keys, query, scores),
             ones[:, part], skip[:, part], tokens, full, column, first_head, count,
         )
-        finals.append(final)
+        incoming.append(entering_state(number, final))
         if number + 2 < len(blocks):
             sent.append(gathered(number + 2, final))
-
-    for (first_head, count, column, width), final in zip(blocks, finals):
-        part = slice(column, column + width)
-        entering = shifted(final.astype(bf16), "seq", 1)
-        for hop in range(shards - 2):
-            outgoing = through[:, part] * entering.astype(f32) + final
-            entering = shifted(outgoing.astype(bf16), "seq", 1)
-        result = correct(result, entry, query, ones[:, part], entering, column)
+        if number == 1:
+            result = corrected(result, 0)
+    for number in range(1, len(blocks)):
+        result = corrected(result, number)
     return result[None]
 
 

time: 295 us -> 302 us (1.024)
  waiting for transfers between devices: 113 us -> 90.6 us
  Pallas kernels: 104 us -> 116 us
  starting transfers between devices: 52.2 us -> 62.9 us
  local copies, waits for them, and re-layouts: 14.3 us -> 20.3 us
    all_to_all x3 -> x4, waiting for transfers between devices: 93.5 us -> 74.5 us  [exchange(): got = lax.all_to_all(block, 'dp', split_axis=0, concat_axis=0, tiled=True)]
    ppermute x9 -> x12, starting transfers between devices: 33.2 us -> 40 us  [shifted(): return lax.ppermute(block, axis, route)]
    pallas_call x3 -> x4, Pallas kernels: 54.2 us -> 59.7 us  [layer(): pl.pallas_call(functools.partial(layer_kernel, spans, first_head, heads,...]
    all_to_all x3 -> x4, starting transfers between devices: 13.9 us -> 17.7 us  [exchange(): got = lax.all_to_all(block, 'dp', split_axis=0, concat_axis=0, tiled=True)]
    pallas_call x3 -> x4, Pallas kernels: 24.2 us -> 27.8 us  [correct(): pl.pallas_call(correct_kernel, grid=(tokens // SPAN,), in_specs=[rows(wid...]
    ppermute x9 -> x12, waiting for transfers between devices: 19.7 us -> 16 us  [shifted(): return lax.ppermute(block, axis, route)]
    slice x2 -> x4, local copies, waits for them, and re-layouts: 3.38 us -> 6.66 us  [on_device(): ones[:, part]]
    pallas_call x3 -> x4, Pallas kernels: 16.3 us -> 19.1 us  [collect(): pl.pallas_call(functools.partial(collect_kernel, groups, capacity, parts)...]
  transfers between devices with their start and end apart: 13 -> 17, of which waited for: 5 -> 5; matrix products, arithmetic and copies ran while one was open for 6% -> 7% of each run, Pallas kernels for 31% -> 34%
where the time goes in v2:
time: 302 us; the launch traced here: 300 us
  Pallas kernels  116 us (38%)
  waiting for transfers between devices  90.6 us (30%)
  starting transfers between devices  62.9 us (21%)
  local copies, waits for them, and re-layouts  20.3 us (7%)
  other arithmetic  9.12 us (3%)
    all_to_all x4, waiting for transfers between devices, exchange(): got = lax.all_to_all(block, 'dp', split_axis=0, concat_axis=0, tiled=True)  74.5 us
    pallas_call x4, Pallas kernels, layer(): pl.pallas_call(functools.partial(layer_kernel, spans, first_head, heads,...  59.7 us
    ppermute x12, starting transfers between devices, shifted(): return lax.ppermute(block, axis, route)  40 us
    pallas_call x4, Pallas kernels, correct(): pl.pallas_call(correct_kernel, grid=(tokens // SPAN,), in_specs=[rows(wid...  27.8 us
    pallas_call x4, Pallas kernels, collect(): pl.pallas_call(functools.partial(collect_kernel, groups, capacity, parts)...  19.1 us
    all_to_all x4, starting transfers between devices, exchange(): got = lax.all_to_all(block, 'dp', split_axis=0, concat_axis=0, tiled=True)  17.7 us
    ppermute x12, waiting for transfers between devices, shifted(): return lax.ppermute(block, axis, route)  16 us
    unnamed x31, local copies, waits for them, and re-layouts  8.33 us
  transfers between devices with their start and end apart: 17, of which 5 were waited for; matrix products, arithmetic and copies ran while one was open for 7% of the time, Pallas kernels for 34%

profile of v2, /device:TPU:0, one launch (start us, length us, event | category | flops | bytes accessed | tf_op | source)
XLA Modules:
  0.0 299.7 jit_solution(13062661641569006806)
XLA Ops:
  1.6 5.2 %all-to-all-start = ((s32[8,1,160]{2,1,0:T(1,128)}), s32[8,1,160]{2,1,0:T(1,128)S(1)}, u32[]{:S(2)}, u32[]{:S(2)}) async-start(s32[8,1,160]{2,1,0:T(1,128)} %broadcast_in_dim.23), calls=%async_computation | async-start | bytes 16384 | tf_op jit(solution)/shard_map/all_to_all | solution.py:421
  6.8 1.1 copy.22
  7.9 1.1 copy.23
  9.0 1.0 fusion.1
  10.6 1.3 copy.24
  12.5 1.6 plan.1
  14.0 6.4 %collect.4.token_ref = bf16[8,21,8,2432]{3,2,1,0:T(8,128)(2,1)} custom-call(s32[8,128]{1,0:T(8,128)} %get-tuple-element.24.send_ref.token_ref, s32[8,128]{1,0:T(8,128)} %get-tuple-element.24.send_ref.token_ref, bf16[160,8,384]{2,1,0:T(8,128)(2,1)} %bitcast.27, bf16[160,8,5120]{2,1,0:T(8,128)(2,1)} %bitcast.22), custom_call_target="tpu_custom_call" | custom-call | bytes 13074432 | tf_op jit(solution)/shard_map/collect/pallas_call | solution.py:116
  20.4 4.8 %all-to-all-start.2 = ((bf16[8,21,8,2432]{3,2,1,0:T(8,128)(2,1)}), bf16[8,21,8,2432]{3,2,1,0:T(8,128)(2,1)}, u32[]{:S(2)}, u32[]{:S(2)}) async-start(bf16[8,21,8,2432]{3,2,1,0:T(8,128)(2,1)} %collect.4.token_ref), calls=%async_computation.2 | async-start | bytes 13074432 | tf_op jit(solution)/shard_map/all_to_all | solution.py:432
  25.2 5.0 %collect.5 = bf16[8,21,8,1536]{3,2,1,0:T(8,128)(2,1)} custom-call(s32[8,128]{1,0:T(8,128)} %get-tuple-element.24.send_ref.token_ref, bf16[8,21,8,2432]{3,2,1,0:T(8,128)(2,1)} %collect.4.token_ref, bf16[160,8,5120]{2,1,0:T(8,128)(2,1)} %bitcast.23), custom_call_target="tpu_custom_call" | custom-call | bytes 8257536 | tf_op jit(solution)/shard_map/collect/pallas_call | solution.py:116
  30.3 69.2 %all-to-all-done.2 = bf16[8,21,8,2432]{3,2,1,0:T(8,128)(2,1)} async-done(((bf16[8,21,8,2432]{3,2,1,0:T(8,128)(2,1)}), bf16[8,21,8,2432]{3,2,1,0:T(8,128)(2,1)}, u32[]{:S(2)}, u32[]{:S(2)}) %all-to-all-start.2) | async-done | bytes 6537248 | tf_op jit(solution)/shard_map/all_to_all | solution.py:432
  99.5 4.5 %all-to-all-start.1 = ((bf16[8,21,8,1536]{3,2,1,0:T(8,128)(2,1)}), bf16[8,21,8,1536]{3,2,1,0:T(8,128)(2,1)}, u32[]{:S(2)}, u32[]{:S(2)}) async-start(bf16[8,21,8,1536]{3,2,1,0:T(8,128)(2,1)} %collect.5), calls=%async_computation.1 | async-start | bytes 8257536 | tf_op jit(solution)/shard_map/all_to_all | solution.py:432
  105.4 1.4 copy-done.2
  106.8 1.1 slice.75.ones_ref
  108.9 8.1 %prepare.1 = (f32[1280,128]{1,0:T(8,128)}, f32[128,1280]{1,0:T(8,128)}, bf16[1280,256]{1,0:T(8,128)(2,1)}, bf16[1280,256]{1,0:T(8,128)(2,1)}, f32[1,128]{1,0:T(1...) custom-call(s32[160]{0:T(256)} %bitcast.35, ...), custom_call_target="tpu_custom_call" | custom-call | tf_op jit(solution)/shard_map/prepare/pallas_call | solution.py:229
  117.0 20.9 %layer.4 = (bf16[1280,5120]{1,0:T(8,128)(2,1)}, f32[128,2048]{1,0:T(8,128)}) custom-call(s32[160]{0:T(256)} %bitcast.36, bf16[168,8,2432]{2,1,0:T(8,128)(2,1)} %bitcast.6.small_ref.values_ref, f32[1280,128]{1,0:T(8,128)} %get-tuple-element.25.cum_ref, f32[128,1280]{1,0:T(8,128)} %get-tuple-element.26.bias_ref, ...), custom_call_target="tpu_custom_call" | custom-call | flops 5368709120 | bytes 10485760 | tf_op jit(solution)/shard_map/layer/pallas_call | solution.py:365
  137.9 1.3 convert_element_type.82
  139.2 3.9 %collective-permute-start = (bf16[128,2048]{1,0:T(8,128)(2,1)S(1)}, bf16[128,2048]{1,0:T(8,128)(2,1)S(1)}, u32[]{:S(2)}, u32[]{:S(2)}) collective-permute-start(bf16[128,2048]{1,0:T(8,128)(2,1)S(1)} %convert_element_type.82), channel_id=1, source_target_pairs={{0,1},{1,2},{2,3},{4,5},{5,6},{6,7},{8,9},{9,10},{10,11},{12,13},{... | collective-permute-start | bytes 1572872 | tf_op jit(solution)/shard_map/ppermute | solution.py:405
  143.1 3.9 %collect.7 = bf16[8,21,8,1024]{3,2,1,0:T(8,128)(2,1)} custom-call(s32[8,128]{1,0:T(8,128)} %get-tuple-element.24.send_ref.token_ref, f32[128,2048]{1,0:T(8,128)} %get-tuple-element.34.token_ref, bf16[160,8,5120]{2,1,0:T(8,128)(2,1)} %bitcast.24), custom_call_target="tpu_custom_call" | custom-call | bytes 5505024 | tf_op jit(solution)/shard_map/collect/pallas_call | solution.py:116
  147.0 5.4 %all-to-all-done.1 = bf16[8,21,8,1536]{3,2,1,0:T(8,128)(2,1)} async-done(((bf16[8,21,8,1536]{3,2,1,0:T(8,128)(2,1)}), bf16[8,21,8,1536]{3,2,1,0:T(8,128)(2,1)}, u32[]{:S(2)}, u32[]{:S(2)}) %all-to-all-start.1) | async-done | bytes 4128800 | tf_op jit(solution)/shard_map/all_to_all | solution.py:432
  152.4 4.4 %all-to-all-start.4 = ((bf16[8,21,8,1024]{3,2,1,0:T(8,128)(2,1)}), bf16[8,21,8,1024]{3,2,1,0:T(8,128)(2,1)}, u32[]{:S(2)}, u32[]{:S(2)}) async-start(bf16[8,21,8,1024]{3,2,1,0:T(8,128)(2,1)} %collect.7), calls=%async_computation.4 | async-start | bytes 5505024 | tf_op jit(solution)/shard_map/all_to_all | solution.py:432
  157.2 3.9 %collective-permute-start.1 = (bf16[128,2048]{1,0:T(8,128)(2,1)S(1)}, bf16[128,2048]{1,0:T(8,128)(2,1)S(1)}, u32[]{:S(2)}, u32[]{:S(2)}) collective-permute-start(bf16[128,2048]{1,0:T(8,128)(2,1)S(1)} %add_convert_fusion.1), channel_id=1, source_target_pairs={{0,1},{1,2},{2,3},{4,5},{5,6},{6,7},{8,9},{9,10},{10,11},{12,13},{... | collective-permute-start | bytes 1572872 | tf_op jit(solution)/shard_map/ppermute | solution.py:405
  161.6 2.1 slice.73.ones_ref
  163.7 9.0 %collective-permute-done.1 = bf16[128,2048]{1,0:T(8,128)(2,1)S(1)} collective-permute-done((bf16[128,2048]{1,0:T(8,128)(2,1)S(1)}, bf16[128,2048]{1,0:T(8,128)(2,1)S(1)}, u32[]{:S(2)}, u32[]{:S(2)}) %collective-permute-start.1) | collective-permute-done | bytes 524320 | tf_op jit(solution)/shard_map/ppermute | solution.py:405
  172.9 4.4 %collective-permute-start.2 = (bf16[128,2048]{1,0:T(8,128)(2,1)S(1)}, bf16[128,2048]{1,0:T(8,128)(2,1)S(1)}, u32[]{:S(2)}, u32[]{:S(2)}) collective-permute-start(bf16[128,2048]{1,0:T(8,128)(2,1)S(1)} %add_convert_fusion), channel_id=1, source_target_pairs={{0,1},{1,2},{2,3},{4,5},{5,6},{6,7},{8,9},{9,10},{10,11},{12,13},{... | collective-permute-start | bytes 1572872 | tf_op jit(solution)/shard_map/ppermute | solution.py:405
  177.3 16.6 %layer.5 = (bf16[1280,5120]{1,0:T(8,128)(2,1)}, f32[128,1536]{1,0:T(8,128)}) custom-call(s32[160]{0:T(256)} %bitcast.37, bf16[168,8,1536]{2,1,0:T(8,128)(2,1)} %bitcast.4.values_ref, f32[1280,128]{1,0:T(8,128)} %get-tuple-element.25.cum_ref, f32[128,1280]{1,0:T(8,128)} %get-tuple-element.26.bias_ref, ...), custom_call_target="tpu_custom_call", output_to_operand_aliasing={{0}: (11, {})} | custom-call | flops 4026531840 | bytes 7864320 | tf_op jit(solution)/shard_map/layer/pallas_call | solution.py:365
  193.9 3.8 %collect.6 = bf16[8,21,8,512]{3,2,1,0:T(8,128)(2,1)} custom-call(s32[8,128]{1,0:T(8,128)} %get-tuple-element.24.send_ref.token_ref, f32[128,1536]{1,0:T(8,128)} %get-tuple-element.33.token_ref, bf16[160,8,5120]{2,1,0:T(8,128)(2,1)} %bitcast.25), custom_call_target="tpu_custom_call" | custom-call | bytes 2752512 | tf_op jit(solution)/shard_map/collect/pallas_call | solution.py:116
  197.7 4.0 %all-to-all-start.3 = ((bf16[8,21,8,512]{3,2,1,0:T(8,128)(2,1)}), bf16[8,21,8,512]{3,2,1,0:T(8,128)(2,1)S(1)}, u32[]{:S(2)}, u32[]{:S(2)}) async-start(bf16[8,21,8,512]{3,2,1,0:T(8,128)(2,1)} %collect.6), calls=%async_computation.3 | async-start | bytes 2752512 | tf_op jit(solution)/shard_map/all_to_all | solution.py:432
  202.3 1.9 slice.79.ones_ref
  205.0 3.7 %collective-permute-start.3 = (bf16[128,1536]{1,0:T(8,128)(2,1)}, bf16[128,1536]{1,0:T(8,128)(2,1)S(1)}, u32[]{:S(2)}, u32[]{:S(2)}) collective-permute-start(bf16[128,1536]{1,0:T(8,128)(2,1)} %convert_element_type.87), channel_id=1, source_target_pairs={{0,1},{1,2},{2,3},{4,5},{5,6},{6,7},{8,9},{9,10},{10,11},{12,13},{... | collective-permute-start | bytes 1179656 | tf_op jit(solution)/shard_map/ppermute | solution.py:405
  209.5 8.9 %correct.4.rest_0_ = bf16[1280,5120]{1,0:T(8,128)(2,1)} custom-call(bf16[1280,5120]{1,0:T(8,128)(2,1)} %get-tuple-element.35.result_ref, bf16[1280,256]{1,0:T(8,128)(2,1)} %get-tuple-element.27.entry_ref, bf16[1280,128]{1,0:T(8,128)(2,1)} %get-tuple-element.30.query_ref, bf16[256,2048]{1,0:T(8,128)(2,1)} %slice.75.ones_ref, ...), custom_call_target="tpu_custom_call", output_to_operand_aliasing={{}: (0, {})} | custom-call | flops 2013265920 | bytes 10485760 | tf_op jit(solution)/shard_map/correct/pallas_call | solution.py:286
  218.3 12.4 %layer.6 = (bf16[1280,5120]{1,0:T(8,128)(2,1)}, f32[128,1024]{1,0:T(8,128)}) custom-call(s32[160]{0:T(256)} %bitcast.38, bf16[168,8,1024]{2,1,0:T(8,128)(2,1)} %bitcast.9.values_ref, f32[1280,128]{1,0:T(8,128)} %get-tuple-element.25.cum_ref, f32[128,1280]{1,0:T(8,128)} %get-tuple-element.26.bias_ref, ...), custom_call_target="tpu_custom_call", output_to_operand_aliasing={{0}: (11, {})} | custom-call | flops 2684354560 | bytes 5242880 | tf_op jit(solution)/shard_map/layer/pallas_call | solution.py:365
  230.8 1.1 convert_element_type.92
  231.8 3.5 %collective-permute-start.6 = (bf16[128,1024]{1,0:T(8,128)(2,1)S(1)}, bf16[128,1024]{1,0:T(8,128)(2,1)S(1)}, u32[]{:S(2)}, u32[]{:S(2)}) collective-permute-start(bf16[128,1024]{1,0:T(8,128)(2,1)S(1)} %convert_element_type.92), channel_id=1, source_target_pairs={{0,1},{1,2},{2,3},{4,5},{5,6},{6,7},{8,9},{9,10},{10,11},{12,13},{... | collective-permute-start | bytes 786440 | tf_op jit(solution)/shard_map/ppermute | solution.py:405
  235.5 1.9 collective-permute-start.4
  237.9 1.7 slice.77.ones_ref
  239.6 1.1 copy-done.3
  240.7 9.8 %layer.7 = (bf16[1280,5120]{1,0:T(8,128)(2,1)}, f32[128,512]{1,0:T(8,128)}) custom-call(s32[160]{0:T(256)} %bitcast.39, bf16[168,8,512]{2,1,0:T(8,128)(2,1)} %bitcast.26, f32[1280,128]{1,0:T(8,128)} %get-tuple-element.25.cum_ref, f32[128,1280]{1,0:T(8,128)} %get-tuple-element.26.bias_ref, ...), custom_call_target="tpu_custom_call", output_to_operand_aliasing={{0}: (11, {})} | custom-call | flops 1342177280 | bytes 2621440 | tf_op jit(solution)/shard_map/layer/pallas_call | solution.py:365
  250.5 1.0 convert_element_type.97
  251.6 1.9 collective-permute-start.9
  253.6 1.9 collective-permute-start.7
  255.6 1.9 collective-permute-start.5
  258.6 4.2 %collective-permute-start.10 = (bf16[128,512]{1,0:T(8,128)(2,1)S(1)}, bf16[128,512]{1,0:T(8,128)(2,1)S(1)}, u32[]{:S(2)}, u32[]{:S(2)}) collective-permute-start(bf16[128,512]{1,0:T(8,128)(2,1)S(1)} %add_convert_fusion.7), channel_id=1, source_target_pairs={{0,1},{1,2},{2,3},{4,5},{5,6},{6,7},{8,9},{9,10},{10,11},{12,13},{... | collective-permute-start | bytes 393224 | tf_op jit(solution)/shard_map/ppermute | solution.py:405
  263.1 4.4 %collective-permute-start.8 = (bf16[128,1024]{1,0:T(8,128)(2,1)S(1)}, bf16[128,1024]{1,0:T(8,128)(2,1)S(1)}, u32[]{:S(2)}, u32[]{:S(2)}) collective-permute-start(bf16[128,1024]{1,0:T(8,128)(2,1)S(1)} %add_convert_fusion.4), channel_id=1, source_target_pairs={{0,1},{1,2},{2,3},{4,5},{5,6},{6,7},{8,9},{9,10},{10,11},{12,13},{... | collective-permute-start | bytes 786440 | tf_op jit(solution)/shard_map/ppermute | solution.py:405
  267.5 6.7 %collective-permute-done.10 = bf16[128,512]{1,0:T(8,128)(2,1)S(1)} collective-permute-done((bf16[128,512]{1,0:T(8,128)(2,1)S(1)}, bf16[128,512]{1,0:T(8,128)(2,1)S(1)}, u32[]{:S(2)}, u32[]{:S(2)}) %collective-permute-start.10) | collective-permute-done | bytes 131104 | tf_op jit(solution)/shard_map/ppermute | solution.py:405
  274.3 4.4 %collective-permute-start.11 = (bf16[128,512]{1,0:T(8,128)(2,1)S(1)}, bf16[128,512]{1,0:T(8,128)(2,1)S(1)}, u32[]{:S(2)}, u32[]{:S(2)}) collective-permute-start(bf16[128,512]{1,0:T(8,128)(2,1)S(1)} %add_convert_fusion.6), channel_id=1, source_target_pairs={{0,1},{1,2},{2,3},{4,5},{5,6},{6,7},{8,9},{9,10},{10,11},{12,13},{... | collective-permute-start | bytes 393224 | tf_op jit(solution)/shard_map/ppermute | solution.py:405
  279.4 7.3 %correct.5.result_ref = bf16[1280,5120]{1,0:T(8,128)(2,1)} custom-call(bf16[1280,5120]{1,0:T(8,128)(2,1)} %get-tuple-element.38.result_ref, bf16[1280,256]{1,0:T(8,128)(2,1)} %get-tuple-element.27.entry_ref, bf16[1280,128]{1,0:T(8,128)(2,1)} %get-tuple-element.30.query_ref, bf16[256,1536]{1,0:T(8,128)(2,1)} %slice.73.ones_ref, ...), custom_call_target="tpu_custom_call", output_to_operand_aliasing={{}: (0, {})} | custom-call | flops 1509949440 | bytes 7864320 | tf_op jit(solution)/shard_map/correct/pallas_call | solution.py:286
  287.4 6.4 %correct.6.result_ref = bf16[1280,5120]{1,0:T(8,128)(2,1)} custom-call(bf16[1280,5120]{1,0:T(8,128)(2,1)} %correct.5.result_ref, bf16[1280,256]{1,0:T(8,128)(2,1)} %get-tuple-element.27.entry_ref, bf16[1280,128]{1,0:T(8,128)(2,1)} %get-tuple-element.30.query_ref, bf16[256,1024]{1,0:T(8,128)(2,1)} %slice.79.ones_ref, ...), custom_call_target="tpu_custom_call", output_to_operand_aliasing={{}: (0, {})} | custom-call | flops 1006632960 | bytes 5242880 | tf_op jit(solution)/shard_map/correct/pallas_call | solution.py:286
  294.5 5.2 %correct.7 = bf16[1280,5120]{1,0:T(8,128)(2,1)} custom-call(bf16[1280,5120]{1,0:T(8,128)(2,1)} %correct.6.result_ref, bf16[1280,256]{1,0:T(8,128)(2,1)} %get-tuple-element.27.entry_ref, bf16[1280,128]{1,0:T(8,128)(2,1)} %get-tuple-element.30.query_ref, bf16[256,512]{1,0:T(8,128)(2,1)} %slice.77.ones_ref, ...), custom_call_target="tpu_custom_call", output_to_operand_aliasing={{}: (0, {})} | custom-call | flops 503316480 | bytes 2621440 | tf_op jit(solution)/shard_map/correct/pallas_call | solution.py:286
  (73 shorter events, 12.5 us)
Async XLA Ops:
  1.6 10.3 %all-to-all-start = ((s32[8,1,160]{2,1,0:T(1,128)}), s32[8,1,160]{2,1,0:T(1,128)S(1)}, u32[]{:S(2)}, u32[]{:S(2)}) async-start(s32[8,1,160]{2,1,0:T(1,128)} %broadcast_in_dim.23), calls=%async_computation | async-start | bytes 16384 | tf_op jit(solution)/shard_map/all_to_all | solution.py:421
  20.4 79.0 %all-to-all-start.2 = ((bf16[8,21,8,2432]{3,2,1,0:T(8,128)(2,1)}), bf16[8,21,8,2432]{3,2,1,0:T(8,128)(2,1)}, u32[]{:S(2)}, u32[]{:S(2)}) async-start(bf16[8,21,8,2432]{3,2,1,0:T(8,128)(2,1)} %collect.4.token_ref), calls=%async_computation.2 | async-start | bytes 13074432 | tf_op jit(solution)/shard_map/all_to_all | solution.py:432
  30.3 73.7 %copy-start.10 = (f32[80]{0:T(128)S(1)}, f32[80]{0:T(128)}, u32[]{:S(2)}) copy-start(f32[80]{0:T(128)} %param.13) | copy-start | bytes 964
  99.5 52.9 %all-to-all-start.1 = ((bf16[8,21,8,1536]{3,2,1,0:T(8,128)(2,1)}), bf16[8,21,8,1536]{3,2,1,0:T(8,128)(2,1)}, u32[]{:S(2)}, u32[]{:S(2)}) async-start(bf16[8,21,8,1536]{3,2,1,0:T(8,128)(2,1)} %collect.5), calls=%async_computation.1 | async-start | bytes 8257536 | tf_op jit(solution)/shard_map/all_to_all | solution.py:432
  104.0 3.9 %copy-start.11 = (f32[80]{0:T(128)S(1)}, f32[80]{0:T(128)}, u32[]{:S(2)}) copy-start(f32[80]{0:T(128)} %param.12) | copy-start | bytes 964
  104.0 4.4 %copy-start.12 = (s32[1,6]{1,0:T(1,128)S(1)}, s32[1,6]{1,0:T(1,128)}, u32[]{:S(2)}) copy-start(s32[1,6]{1,0:T(1,128)} %param.15) | copy-start | bytes 76
  105.4 1.5 copy-start.2
  139.2 17.8 %collective-permute-start = (bf16[128,2048]{1,0:T(8,128)(2,1)S(1)}, bf16[128,2048]{1,0:T(8,128)(2,1)S(1)}, u32[]{:S(2)}, u32[]{:S(2)}) collective-permute-start(bf16[128,2048]{1,0:T(8,128)(2,1)S(1)} %convert_element_type.82), channel_id=1, source_target_pairs={{0,1},{1,2},{2,3},{4,5},{5,6},{6,7},{8,9},{9,10},{10,11},{12,13},{... | collective-permute-start | bytes 1572872 | tf_op jit(solution)/shard_map/ppermute | solution.py:405
  147.0 9.8 %copy-start.13 = (f32[1,128]{1,0:T(1,128)S(1)}, f32[1,128]{1,0:T(1,128)}, u32[]{:S(2)}) copy-start(f32[1,128]{1,0:T(1,128)} %get-tuple-element.36) | copy-start | bytes 1540
  147.0 10.0 %copy-start = (f32[128,2048]{1,0:T(8,128)S(1)}, f32[128,2048]{1,0:T(8,128)}, u32[]{:S(2)}) copy-start(f32[128,2048]{1,0:T(8,128)} %get-tuple-element.34.token_ref) | copy-start | bytes 3145732
  152.4 45.3 %all-to-all-start.4 = ((bf16[8,21,8,1024]{3,2,1,0:T(8,128)(2,1)}), bf16[8,21,8,1024]{3,2,1,0:T(8,128)(2,1)}, u32[]{:S(2)}, u32[]{:S(2)}) async-start(bf16[8,21,8,1024]{3,2,1,0:T(8,128)(2,1)} %collect.7), calls=%async_computation.4 | async-start | bytes 5505024 | tf_op jit(solution)/shard_map/all_to_all | solution.py:432
  157.2 15.5 %collective-permute-start.1 = (bf16[128,2048]{1,0:T(8,128)(2,1)S(1)}, bf16[128,2048]{1,0:T(8,128)(2,1)S(1)}, u32[]{:S(2)}, u32[]{:S(2)}) collective-permute-start(bf16[128,2048]{1,0:T(8,128)(2,1)S(1)} %add_convert_fusion.1), channel_id=1, source_target_pairs={{0,1},{1,2},{2,3},{4,5},{5,6},{6,7},{8,9},{9,10},{10,11},{12,13},{... | collective-permute-start | bytes 1572872 | tf_op jit(solution)/shard_map/ppermute | solution.py:405
  172.9 35.8 %collective-permute-start.2 = (bf16[128,2048]{1,0:T(8,128)(2,1)S(1)}, bf16[128,2048]{1,0:T(8,128)(2,1)S(1)}, u32[]{:S(2)}, u32[]{:S(2)}) collective-permute-start(bf16[128,2048]{1,0:T(8,128)(2,1)S(1)} %add_convert_fusion), channel_id=1, source_target_pairs={{0,1},{1,2},{2,3},{4,5},{5,6},{6,7},{8,9},{9,10},{10,11},{12,13},{... | collective-permute-start | bytes 1572872 | tf_op jit(solution)/shard_map/ppermute | solution.py:405
  197.7 6.5 %copy-start.1 = (f32[128,1536]{1,0:T(8,128)S(1)}, f32[128,1536]{1,0:T(8,128)}, u32[]{:S(2)}) copy-start(f32[128,1536]{1,0:T(8,128)} %get-tuple-element.33.token_ref) | copy-start | bytes 2359300
  197.7 41.9 %all-to-all-start.3 = ((bf16[8,21,8,512]{3,2,1,0:T(8,128)(2,1)}), bf16[8,21,8,512]{3,2,1,0:T(8,128)(2,1)S(1)}, u32[]{:S(2)}, u32[]{:S(2)}) async-start(bf16[8,21,8,512]{3,2,1,0:T(8,128)(2,1)} %collect.6), calls=%async_computation.3 | async-start | bytes 2752512 | tf_op jit(solution)/shard_map/all_to_all | solution.py:432
  205.0 30.4 %collective-permute-start.3 = (bf16[128,1536]{1,0:T(8,128)(2,1)}, bf16[128,1536]{1,0:T(8,128)(2,1)S(1)}, u32[]{:S(2)}, u32[]{:S(2)}) collective-permute-start(bf16[128,1536]{1,0:T(8,128)(2,1)} %convert_element_type.87), channel_id=1, source_target_pairs={{0,1},{1,2},{2,3},{4,5},{5,6},{6,7},{8,9},{9,10},{10,11},{12,13},{... | collective-permute-start | bytes 1179656 | tf_op jit(solution)/shard_map/ppermute | solution.py:405
  208.7 0.8 copy-start.6
  231.8 21.7 %collective-permute-start.6 = (bf16[128,1024]{1,0:T(8,128)(2,1)S(1)}, bf16[128,1024]{1,0:T(8,128)(2,1)S(1)}, u32[]{:S(2)}, u32[]{:S(2)}) collective-permute-start(bf16[128,1024]{1,0:T(8,128)(2,1)S(1)} %convert_element_type.92), channel_id=1, source_target_pairs={{0,1},{1,2},{2,3},{4,5},{5,6},{6,7},{8,9},{9,10},{10,11},{12,13},{... | collective-permute-start | bytes 786440 | tf_op jit(solution)/shard_map/ppermute | solution.py:405
  235.5 20.1 %collective-permute-start.4 = (bf16[128,1536]{1,0:T(8,128)(2,1)S(1)}, bf16[128,1536]{1,0:T(8,128)(2,1)S(1)}, u32[]{:S(2)}, u32[]{:S(2)}) collective-permute-start(bf16[128,1536]{1,0:T(8,128)(2,1)S(1)} %add_convert_fusion.3), channel_id=1, source_target_pairs={{0,1},{1,2},{2,3},{4,5},{5,6},{6,7},{8,9},{9,10},{10,11},{12,13},{... | collective-permute-start | bytes 1179656 | tf_op jit(solution)/shard_map/ppermute | solution.py:405
  239.6 1.1 copy-start.3
  240.7 12.8 %copy-start.4 = (f32[128,1024]{1,0:T(8,128)S(1)}, f32[128,1024]{1,0:T(8,128)}, u32[]{:S(2)}) copy-start(f32[128,1024]{1,0:T(8,128)} %get-tuple-element.39) | copy-start | bytes 1572868
  250.5 23.7 %copy-start.5 = (f32[128,512]{1,0:T(8,128)S(1)}, f32[128,512]{1,0:T(8,128)}, u32[]{:S(2)}) copy-start(f32[128,512]{1,0:T(8,128)} %get-tuple-element.40) | copy-start | bytes 786436
  251.6 6.0 %collective-permute-start.9 = (bf16[128,512]{1,0:T(8,128)(2,1)S(1)}, bf16[128,512]{1,0:T(8,128)(2,1)S(1)}, u32[]{:S(2)}, u32[]{:S(2)}) collective-permute-start(bf16[128,512]{1,0:T(8,128)(2,1)S(1)} %convert_element_type.97), channel_id=1, source_target_pairs={{0,1},{1,2},{2,3},{4,5},{5,6},{6,7},{8,9},{9,10},{10,11},{12,13},{... | collective-permute-start | bytes 393224 | tf_op jit(solution)/shard_map/ppermute | solution.py:405
  253.6 9.4 %collective-permute-start.7 = (bf16[128,1024]{1,0:T(8,128)(2,1)S(1)}, bf16[128,1024]{1,0:T(8,128)(2,1)S(1)}, u32[]{:S(2)}, u32[]{:S(2)}) collective-permute-start(bf16[128,1024]{1,0:T(8,128)(2,1)S(1)} %add_convert_fusion.5), channel_id=1, source_target_pairs={{0,1},{1,2},{2,3},{4,5},{5,6},{6,7},{8,9},{9,10},{10,11},{12,13},{... | collective-permute-start | bytes 786440 | tf_op jit(solution)/shard_map/ppermute | solution.py:405
  255.6 23.0 %collective-permute-start.5 = (bf16[128,1536]{1,0:T(8,128)(2,1)S(1)}, bf16[128,1536]{1,0:T(8,128)(2,1)S(1)}, u32[]{:S(2)}, u32[]{:S(2)}) collective-permute-start(bf16[128,1536]{1,0:T(8,128)(2,1)S(1)} %add_convert_fusion.2), channel_id=1, source_target_pairs={{0,1},{1,2},{2,3},{4,5},{5,6},{6,7},{8,9},{9,10},{10,11},{12,13},{... | collective-permute-start | bytes 1179656 | tf_op jit(solution)/shard_map/ppermute | solution.py:405
  258.6 15.6 %collective-permute-start.10 = (bf16[128,512]{1,0:T(8,128)(2,1)S(1)}, bf16[128,512]{1,0:T(8,128)(2,1)S(1)}, u32[]{:S(2)}, u32[]{:S(2)}) collective-permute-start(bf16[128,512]{1,0:T(8,128)(2,1)S(1)} %add_convert_fusion.7), channel_id=1, source_target_pairs={{0,1},{1,2},{2,3},{4,5},{5,6},{6,7},{8,9},{9,10},{10,11},{12,13},{... | collective-permute-start | bytes 393224 | tf_op jit(solution)/shard_map/ppermute | solution.py:405
  263.1 23.7 %collective-permute-start.8 = (bf16[128,1024]{1,0:T(8,128)(2,1)S(1)}, bf16[128,1024]{1,0:T(8,128)(2,1)S(1)}, u32[]{:S(2)}, u32[]{:S(2)}) collective-permute-start(bf16[128,1024]{1,0:T(8,128)(2,1)S(1)} %add_convert_fusion.4), channel_id=1, source_target_pairs={{0,1},{1,2},{2,3},{4,5},{5,6},{6,7},{8,9},{9,10},{10,11},{12,13},{... | collective-permute-start | bytes 786440 | tf_op jit(solution)/shard_map/ppermute | solution.py:405
  274.3 19.6 %collective-permute-start.11 = (bf16[128,512]{1,0:T(8,128)(2,1)S(1)}, bf16[128,512]{1,0:T(8,128)(2,1)S(1)}, u32[]{:S(2)}, u32[]{:S(2)}) collective-permute-start(bf16[128,512]{1,0:T(8,128)(2,1)S(1)} %add_convert_fusion.6), channel_id=1, source_target_pairs={{0,1},{1,2},{2,3},{4,5},{5,6},{6,7},{8,9},{9,10},{10,11},{12,13},{... | collective-permute-start | bytes 393224 | tf_op jit(solution)/shard_map/ppermute | solution.py:405
  278.7 0.8 copy-start.7
  286.7 0.7 copy-start.8
  293.9 0.7 copy-start.9

commit v3 on v2

--- a/solution.py
+++ b/solution.py
@@ -395,8 +395,8 @@
 
 
 def chunk_plan(heads):
-    unit = heads // 10
-    return ((4 * unit, 4 * unit), (0, 3 * unit), (8 * unit, 2 * unit), (3 * unit, unit))
+    unit = heads // 4
+    return ((0, unit), (2 * unit, 2 * unit), (unit, unit))
 
 
 def shifted(block, axis, distance):
@@ -486,7 +486,7 @@
         incoming.append(entering_state(number, final))
         if number + 2 < len(blocks):
             sent.append(gathered(number + 2, final))
-        if number == 1:
+        if number == 0:
             result = corrected(result, 0)
     for number in range(1, len(blocks)):
         result = corrected(result, number)

time: 302 us -> 311 us (1.030)
  waiting for transfers between devices: 90.6 us -> 122 us
  Pallas kernels: 116 us -> 103 us
  starting transfers between devices: 62.9 us -> 55.3 us
  local copies, waits for them, and re-layouts: 20.3 us -> 15.1 us
  other arithmetic: 9.12 us -> 13.2 us
    ppermute x12 -> x9, waiting for transfers between devices: 16 us -> 36.6 us  [shifted(): return lax.ppermute(block, axis, route)]
    all_to_all x4 -> x3, waiting for transfers between devices: 74.5 us -> 85.2 us  [exchange(): got = lax.all_to_all(block, 'dp', split_axis=0, concat_axis=0, tiled=True)]
    pallas_call x4 -> x3, Pallas kernels: 59.7 us -> 54.4 us  [layer(): pl.pallas_call(functools.partial(layer_kernel, spans, first_head, heads,...]
    pallas_call x4 -> x3, Pallas kernels: 27.8 us -> 23 us  [correct(): pl.pallas_call(correct_kernel, grid=(tokens // SPAN,), in_specs=[rows(wid...]
    all_to_all x4 -> x3, starting transfers between devices: 17.7 us -> 13.1 us  [exchange(): got = lax.all_to_all(block, 'dp', split_axis=0, concat_axis=0, tiled=True)]
    slice x4 -> x2, local copies, waits for them, and re-layouts: 6.66 us -> 2.41 us  [on_device(): ones[:, part]]
    pallas_call x4 -> x3, Pallas kernels: 19.1 us -> 15.8 us  [collect(): pl.pallas_call(functools.partial(collect_kernel, groups, capacity, parts)...]
    ppermute x12 -> x9, starting transfers between devices: 40 us -> 37 us  [shifted(): return lax.ppermute(block, axis, route)]
  transfers between devices with their start and end apart: 17 -> 13, of which waited for: 5 -> 8; matrix products, arithmetic and copies ran while one was open for 7% -> 7% of each run, Pallas kernels for 34% -> 29%
where the time goes in v3:
time: 311 us; the launch traced here: 309 us
  waiting for transfers between devices  122 us (39%)
  Pallas kernels  103 us (33%)
  starting transfers between devices  55.3 us (18%)
  local copies, waits for them, and re-layouts  15.1 us (5%)
  other arithmetic  13.2 us (4%)
    all_to_all x3, waiting for transfers between devices, exchange(): got = lax.all_to_all(block, 'dp', split_axis=0, concat_axis=0, tiled=True)  85.2 us
    pallas_call x3, Pallas kernels, layer(): pl.pallas_call(functools.partial(layer_kernel, spans, first_head, heads,...  54.4 us
    ppermute x9, starting transfers between devices, shifted(): return lax.ppermute(block, axis, route)  37 us
    ppermute x9, waiting for transfers between devices, shifted(): return lax.ppermute(block, axis, route)  36.6 us
    pallas_call x3, Pallas kernels, correct(): pl.pallas_call(correct_kernel, grid=(tokens // SPAN,), in_specs=[rows(wid...  23 us
    pallas_call x3, Pallas kernels, collect(): pl.pallas_call(functools.partial(collect_kernel, groups, capacity, parts)...  15.8 us
    all_to_all x3, starting transfers between devices, exchange(): got = lax.all_to_all(block, 'dp', split_axis=0, concat_axis=0, tiled=True)  13.1 us
    unnamed x27, local copies, waits for them, and re-layouts  8.42 us
  transfers between devices with their start and end apart: 13, of which 8 were waited for; matrix products, arithmetic and copies ran while one was open for 7% of the time, Pallas kernels for 29%

profile of v3, /device:TPU:0, one launch (start us, length us, event | category | flops | bytes accessed | tf_op | source)
XLA Modules:
  0.0 308.8 jit_solution(7979552544975477062)
XLA Ops:
  1.6 5.2 %all-to-all-start = ((s32[8,1,160]{2,1,0:T(1,128)}), s32[8,1,160]{2,1,0:T(1,128)S(1)}, u32[]{:S(2)}, u32[]{:S(2)}) async-start(s32[8,1,160]{2,1,0:T(1,128)} %broadcast_in_dim.23), calls=%async_computation | async-start | bytes 16384 | tf_op jit(solution)/shard_map/all_to_all | solution.py:421
  6.8 1.1 copy.20
  7.9 1.1 copy.21
  9.0 1.0 fusion.1
  10.6 1.3 copy.22
  12.6 1.6 plan.1
  14.1 5.1 %collect.3.token_ref = bf16[8,21,8,1664]{3,2,1,0:T(8,128)(2,1)} custom-call(s32[8,128]{1,0:T(8,128)} %get-tuple-element.22.send_ref.token_ref, s32[8,128]{1,0:T(8,128)} %get-tuple-element.22.send_ref.token_ref, bf16[160,8,384]{2,1,0:T(8,128)(2,1)} %bitcast.22, bf16[160,8,5120]{2,1,0:T(8,128)(2,1)} %bitcast.18), custom_call_target="tpu_custom_call" | custom-call | bytes 8945664 | tf_op jit(solution)/shard_map/collect/pallas_call | solution.py:116
  19.2 4.6 %all-to-all-start.1 = ((bf16[8,21,8,1664]{3,2,1,0:T(8,128)(2,1)}), bf16[8,21,8,1664]{3,2,1,0:T(8,128)(2,1)}, u32[]{:S(2)}, u32[]{:S(2)}) async-start(bf16[8,21,8,1664]{3,2,1,0:T(8,128)(2,1)} %collect.3.token_ref), calls=%async_computation.1 | async-start | bytes 8945664 | tf_op jit(solution)/shard_map/all_to_all | solution.py:432
  23.8 6.6 %collect.5 = bf16[8,21,8,2560]{3,2,1,0:T(8,128)(2,1)} custom-call(s32[8,128]{1,0:T(8,128)} %get-tuple-element.22.send_ref.token_ref, bf16[8,21,8,1664]{3,2,1,0:T(8,128)(2,1)} %collect.3.token_ref, bf16[160,8,5120]{2,1,0:T(8,128)(2,1)} %bitcast.19), custom_call_target="tpu_custom_call" | custom-call | bytes 13762560 | tf_op jit(solution)/shard_map/collect/pallas_call | solution.py:116
  30.5 45.5 %all-to-all-done.1 = bf16[8,21,8,1664]{3,2,1,0:T(8,128)(2,1)} async-done(((bf16[8,21,8,1664]{3,2,1,0:T(8,128)(2,1)}), bf16[8,21,8,1664]{3,2,1,0:T(8,128)(2,1)}, u32[]{:S(2)}, u32[]{:S(2)}) %all-to-all-start.1) | async-done | bytes 4472864 | tf_op jit(solution)/shard_map/all_to_all | solution.py:432
  76.0 4.8 %all-to-all-start.3 = ((bf16[8,21,8,2560]{3,2,1,0:T(8,128)(2,1)}), bf16[8,21,8,2560]{3,2,1,0:T(8,128)(2,1)}, u32[]{:S(2)}, u32[]{:S(2)}) async-start(bf16[8,21,8,2560]{3,2,1,0:T(8,128)(2,1)} %collect.5), calls=%async_computation.3 | async-start | bytes 13762560 | tf_op jit(solution)/shard_map/all_to_all | solution.py:432
  83.3 1.5 copy-done.2
  84.7 1.2 fusion.5
  85.9 8.2 %prepare.1 = (f32[1280,128]{1,0:T(8,128)}, f32[128,1280]{1,0:T(8,128)}, bf16[1280,256]{1,0:T(8,128)(2,1)}, bf16[1280,256]{1,0:T(8,128)(2,1)}, f32[1,128]{1,0:T(1...) custom-call(s32[160]{0:T(256)} %bitcast.25, ...), custom_call_target="tpu_custom_call" | custom-call | tf_op jit(solution)/shard_map/prepare/pallas_call | solution.py:229
  94.2 14.6 %layer.3 = (bf16[1280,5120]{1,0:T(8,128)(2,1)}, f32[128,1280]{1,0:T(8,128)}) custom-call(s32[160]{0:T(256)} %bitcast.26, bf16[168,8,1664]{2,1,0:T(8,128)(2,1)} %bitcast.4.small_ref.values_ref, f32[1280,128]{1,0:T(8,128)} %get-tuple-element.23.cum_ref, f32[128,1280]{1,0:T(8,128)} %get-tuple-element.24.bias_ref, ...), custom_call_target="tpu_custom_call" | custom-call | flops 3355443200 | bytes 6553600 | tf_op jit(solution)/shard_map/layer/pallas_call | solution.py:365
  108.8 1.8 convert_element_type.63
  110.7 4.1 %collect.4 = bf16[8,21,8,1280]{3,2,1,0:T(8,128)(2,1)} custom-call(s32[8,128]{1,0:T(8,128)} %get-tuple-element.22.send_ref.token_ref, f32[128,1280]{1,0:T(8,128)} %get-tuple-element.30.token_ref, bf16[160,8,5120]{2,1,0:T(8,128)(2,1)} %bitcast.20), custom_call_target="tpu_custom_call" | custom-call | bytes 6881280 | tf_op jit(solution)/shard_map/collect/pallas_call | solution.py:116
  114.7 4.2 %collective-permute-start = (bf16[128,1280]{1,0:T(8,128)(2,1)}, bf16[128,1280]{1,0:T(8,128)(2,1)}, u32[]{:S(2)}, u32[]{:S(2)}) collective-permute-start(bf16[128,1280]{1,0:T(8,128)(2,1)} %convert_element_type.63), channel_id=1, source_target_pairs={{0,1},{1,2},{2,3},{4,5},{5,6},{6,7},{8,9},{9,10},{10,11},{12,13},{... | collective-permute-start | bytes 983048 | tf_op jit(solution)/shard_map/ppermute | solution.py:405
  119.0 39.7 %all-to-all-done.3 = bf16[8,21,8,2560]{3,2,1,0:T(8,128)(2,1)} async-done(((bf16[8,21,8,2560]{3,2,1,0:T(8,128)(2,1)}), bf16[8,21,8,2560]{3,2,1,0:T(8,128)(2,1)}, u32[]{:S(2)}, u32[]{:S(2)}) %all-to-all-start.3) | async-done | bytes 6881312 | tf_op jit(solution)/shard_map/all_to_all | solution.py:432
  158.7 3.7 %all-to-all-start.2 = ((bf16[8,21,8,1280]{3,2,1,0:T(8,128)(2,1)}), bf16[8,21,8,1280]{3,2,1,0:T(8,128)(2,1)S(1)}, u32[]{:S(2)}, u32[]{:S(2)}) async-start(bf16[8,21,8,1280]{3,2,1,0:T(8,128)(2,1)} %collect.4), calls=%async_computation.2 | async-start | bytes 6881280 | tf_op jit(solution)/shard_map/all_to_all | solution.py:432
  162.6 1.4 add_convert_fusion.5
  164.0 3.5 %collective-permute-start.1 = (bf16[128,1280]{1,0:T(8,128)(2,1)S(1)}, bf16[128,1280]{1,0:T(8,128)(2,1)S(1)}, u32[]{:S(2)}, u32[]{:S(2)}) collective-permute-start(bf16[128,1280]{1,0:T(8,128)(2,1)S(1)} %add_convert_fusion.5), channel_id=1, source_target_pairs={{0,1},{1,2},{2,3},{4,5},{5,6},{6,7},{8,9},{9,10},{10,11},{12,13},{... | collective-permute-start | bytes 983048 | tf_op jit(solution)/shard_map/ppermute | solution.py:405
  167.6 7.5 %collective-permute-done.1 = bf16[128,1280]{1,0:T(8,128)(2,1)S(1)} collective-permute-done((bf16[128,1280]{1,0:T(8,128)(2,1)S(1)}, bf16[128,1280]{1,0:T(8,128)(2,1)S(1)}, u32[]{:S(2)}, u32[]{:S(2)}) %collective-permute-start.1) | collective-permute-done | bytes 327712 | tf_op jit(solution)/shard_map/ppermute | solution.py:405
  175.0 1.2 add_convert_fusion.4
  176.2 4.4 %collective-permute-start.2 = (bf16[128,1280]{1,0:T(8,128)(2,1)S(1)}, bf16[128,1280]{1,0:T(8,128)(2,1)S(1)}, u32[]{:S(2)}, u32[]{:S(2)}) collective-permute-start(bf16[128,1280]{1,0:T(8,128)(2,1)S(1)} %add_convert_fusion.4), channel_id=1, source_target_pairs={{0,1},{1,2},{2,3},{4,5},{5,6},{6,7},{8,9},{9,10},{10,11},{12,13},{... | collective-permute-start | bytes 983048 | tf_op jit(solution)/shard_map/ppermute | solution.py:405
  181.2 1.2 slice.61.ones_ref
  182.4 4.8 %collective-permute-done.2.incoming_ref = bf16[128,1280]{1,0:T(8,128)(2,1)S(1)} collective-permute-done((bf16[128,1280]{1,0:T(8,128)(2,1)S(1)}, bf16[128,1280]{1,0:T(8,128)(2,1)S(1)}, u32[]{:S(2)}, u32[]{:S(2)}) %collective-permute-start.2) | collective-permute-done | bytes 327712 | tf_op jit(solution)/shard_map/ppermute | solution.py:405
  188.0 6.7 %correct.3.rest_0_ = bf16[1280,5120]{1,0:T(8,128)(2,1)} custom-call(bf16[1280,5120]{1,0:T(8,128)(2,1)} %get-tuple-element.31.result_ref, bf16[1280,256]{1,0:T(8,128)(2,1)} %get-tuple-element.25.entry_ref, bf16[1280,128]{1,0:T(8,128)(2,1)} %get-tuple-element.28.query_ref, ...), custom_call_target="tpu_custom_call", output_to_operand_aliasing={{}: (0, {})} | custom-call | flops 1258291200 | bytes 6553600 | tf_op jit(solution)/shard_map/correct/pallas_call | solution.py:286
  194.7 25.2 %layer.4 = (bf16[1280,5120]{1,0:T(8,128)(2,1)}, f32[128,2560]{1,0:T(8,128)}) custom-call(s32[160]{0:T(256)} %bitcast.27, bf16[168,8,2560]{2,1,0:T(8,128)(2,1)} %bitcast.8.values_ref, f32[1280,128]{1,0:T(8,128)} %get-tuple-element.23.cum_ref, f32[128,1280]{1,0:T(8,128)} %get-tuple-element.24.bias_ref, ...), custom_call_target="tpu_custom_call", output_to_operand_aliasing={{0}: (11, {})} | custom-call | flops 6710886400 | bytes 13107200 | tf_op jit(solution)/shard_map/layer/pallas_call | solution.py:365
  219.9 2.2 convert_element_type.68
  222.1 5.2 %collective-permute-start.3 = (bf16[128,2560]{1,0:T(8,128)(2,1)}, bf16[128,2560]{1,0:T(8,128)(2,1)}, u32[]{:S(2)}, u32[]{:S(2)}) collective-permute-start(bf16[128,2560]{1,0:T(8,128)(2,1)} %convert_element_type.68), channel_id=1, source_target_pairs={{0,1},{1,2},{2,3},{4,5},{5,6},{6,7},{8,9},{9,10},{10,11},{12,13},{... | collective-permute-start | bytes 1966088 | tf_op jit(solution)/shard_map/ppermute | solution.py:405
  227.4 1.7 copy-done
  229.1 14.6 %layer.5 = (bf16[1280,5120]{1,0:T(8,128)(2,1)}, f32[128,1280]{1,0:T(8,128)}) custom-call(s32[160]{0:T(256)} %bitcast.28, bf16[168,8,1280]{2,1,0:T(8,128)(2,1)} %bitcast.21, f32[1280,128]{1,0:T(8,128)} %get-tuple-element.23.cum_ref, f32[128,1280]{1,0:T(8,128)} %get-tuple-element.24.bias_ref, ...), custom_call_target="tpu_custom_call", output_to_operand_aliasing={{0}: (11, {})} | custom-call | flops 3355443200 | bytes 6553600 | tf_op jit(solution)/shard_map/layer/pallas_call | solution.py:365
  243.7 1.2 convert_element_type.73
  244.9 3.0 collective-permute-start.6
  248.0 1.6 add_convert_fusion.1
  249.7 3.4 %collective-permute-start.4 = (bf16[128,2560]{1,0:T(8,128)(2,1)S(1)}, bf16[128,2560]{1,0:T(8,128)(2,1)S(1)}, u32[]{:S(2)}, u32[]{:S(2)}) collective-permute-start(bf16[128,2560]{1,0:T(8,128)(2,1)S(1)} %add_convert_fusion.1), channel_id=1, source_target_pairs={{0,1},{1,2},{2,3},{4,5},{5,6},{6,7},{8,9},{9,10},{10,11},{12,13},{... | collective-permute-start | bytes 1966088 | tf_op jit(solution)/shard_map/ppermute | solution.py:405
  253.0 2.8 collective-permute-done.6
  255.9 4.4 %collective-permute-start.7 = (bf16[128,1280]{1,0:T(8,128)(2,1)S(1)}, bf16[128,1280]{1,0:T(8,128)(2,1)S(1)}, u32[]{:S(2)}, u32[]{:S(2)}) collective-permute-start(bf16[128,1280]{1,0:T(8,128)(2,1)S(1)} %add_convert_fusion.3), channel_id=1, source_target_pairs={{0,1},{1,2},{2,3},{4,5},{5,6},{6,7},{8,9},{9,10},{10,11},{12,13},{... | collective-permute-start | bytes 983048 | tf_op jit(solution)/shard_map/ppermute | solution.py:405
  260.3 9.5 %collective-permute-done.4 = bf16[128,2560]{1,0:T(8,128)(2,1)S(1)} collective-permute-done((bf16[128,2560]{1,0:T(8,128)(2,1)S(1)}, bf16[128,2560]{1,0:T(8,128)(2,1)S(1)}, u32[]{:S(2)}, u32[]{:S(2)}) %collective-permute-start.4) | collective-permute-done | bytes 655392 | tf_op jit(solution)/shard_map/ppermute | solution.py:405
  270.0 4.4 %collective-permute-start.5 = (bf16[128,2560]{1,0:T(8,128)(2,1)S(1)}, bf16[128,2560]{1,0:T(8,128)(2,1)S(1)}, u32[]{:S(2)}, u32[]{:S(2)}) collective-permute-start(bf16[128,2560]{1,0:T(8,128)(2,1)S(1)} %add_convert_fusion), channel_id=1, source_target_pairs={{0,1},{1,2},{2,3},{4,5},{5,6},{6,7},{8,9},{9,10},{10,11},{12,13},{... | collective-permute-start | bytes 1966088 | tf_op jit(solution)/shard_map/ppermute | solution.py:405
  274.4 2.4 collective-permute-done.7
  276.9 4.4 %collective-permute-start.8 = (bf16[128,1280]{1,0:T(8,128)(2,1)S(1)}, bf16[128,1280]{1,0:T(8,128)(2,1)S(1)}, u32[]{:S(2)}, u32[]{:S(2)}) collective-permute-start(bf16[128,1280]{1,0:T(8,128)(2,1)S(1)} %add_convert_fusion.2), channel_id=1, source_target_pairs={{0,1},{1,2},{2,3},{4,5},{5,6},{6,7},{8,9},{9,10},{10,11},{12,13},{... | collective-permute-start | bytes 983048 | tf_op jit(solution)/shard_map/ppermute | solution.py:405
  281.4 9.5 %collective-permute-done.5.incoming_ref = bf16[128,2560]{1,0:T(8,128)(2,1)S(1)} collective-permute-done((bf16[128,2560]{1,0:T(8,128)(2,1)S(1)}, bf16[128,2560]{1,0:T(8,128)(2,1)S(1)}, u32[]{:S(2)}, u32[]{:S(2)}) %collective-permute-start.5) | collective-permute-done | bytes 655392 | tf_op jit(solution)/shard_map/ppermute | solution.py:405
  290.9 0.9 copy-done.5
  291.8 9.6 %correct.4.result_ref = bf16[1280,5120]{1,0:T(8,128)(2,1)} custom-call(bf16[1280,5120]{1,0:T(8,128)(2,1)} %get-tuple-element.34.result_ref, bf16[1280,256]{1,0:T(8,128)(2,1)} %get-tuple-element.25.entry_ref, bf16[1280,128]{1,0:T(8,128)(2,1)} %get-tuple-element.28.query_ref, bf16[256,2560]{1,0:T(8,128)(2,1)} %slice.61.ones_ref, ...), custom_call_target="tpu_custom_call", output_to_operand_aliasing={{}: (0, {})} | custom-call | flops 2516582400 | bytes 13107200 | tf_op jit(solution)/shard_map/correct/pallas_call | solution.py:286
  301.3 0.8 copy-done.6
  302.1 6.7 %correct.5 = bf16[1280,5120]{1,0:T(8,128)(2,1)} custom-call(bf16[1280,5120]{1,0:T(8,128)(2,1)} %correct.4.result_ref, bf16[1280,256]{1,0:T(8,128)(2,1)} %get-tuple-element.25.entry_ref, bf16[1280,128]{1,0:T(8,128)(2,1)} %get-tuple-element.28.query_ref, bf16[256,1280]{1,0:T(8,128)(2,1)} %get-tuple-element.39.ones_ref, ...), custom_call_target="tpu_custom_call", output_to_operand_aliasing={{}: (0, {})} | custom-call | flops 1258291200 | bytes 6553600 | tf_op jit(solution)/shard_map/correct/pallas_call | solution.py:286
  (49 shorter events, 7.0 us)
Async XLA Ops:
  1.6 10.4 %all-to-all-start = ((s32[8,1,160]{2,1,0:T(1,128)}), s32[8,1,160]{2,1,0:T(1,128)S(1)}, u32[]{:S(2)}, u32[]{:S(2)}) async-start(s32[8,1,160]{2,1,0:T(1,128)} %broadcast_in_dim.23), calls=%async_computation | async-start | bytes 16384 | tf_op jit(solution)/shard_map/all_to_all | solution.py:421
  19.2 56.8 %all-to-all-start.1 = ((bf16[8,21,8,1664]{3,2,1,0:T(8,128)(2,1)}), bf16[8,21,8,1664]{3,2,1,0:T(8,128)(2,1)}, u32[]{:S(2)}, u32[]{:S(2)}) async-start(bf16[8,21,8,1664]{3,2,1,0:T(8,128)(2,1)} %collect.3.token_ref), calls=%async_computation.1 | async-start | bytes 8945664 | tf_op jit(solution)/shard_map/all_to_all | solution.py:432
  30.5 50.3 %copy-start.8 = (f32[80]{0:T(128)S(1)}, f32[80]{0:T(128)}, u32[]{:S(2)}) copy-start(f32[80]{0:T(128)} %param.13) | copy-start | bytes 964
  30.5 50.5 %copy-start.9 = (f32[80]{0:T(128)S(1)}, f32[80]{0:T(128)}, u32[]{:S(2)}) copy-start(f32[80]{0:T(128)} %param.12) | copy-start | bytes 964
  30.5 51.1 %copy-start.10 = (s32[1,6]{1,0:T(1,128)S(1)}, s32[1,6]{1,0:T(1,128)}, u32[]{:S(2)}) copy-start(s32[1,6]{1,0:T(1,128)} %param.15) | copy-start | bytes 76
  76.0 82.7 %all-to-all-start.3 = ((bf16[8,21,8,2560]{3,2,1,0:T(8,128)(2,1)}), bf16[8,21,8,2560]{3,2,1,0:T(8,128)(2,1)}, u32[]{:S(2)}, u32[]{:S(2)}) async-start(bf16[8,21,8,2560]{3,2,1,0:T(8,128)(2,1)} %collect.5), calls=%async_computation.3 | async-start | bytes 13762560 | tf_op jit(solution)/shard_map/all_to_all | solution.py:432
  83.2 1.5 copy-start.2
  114.7 47.6 %copy-start.11 = (f32[1,128]{1,0:T(1,128)S(1)}, f32[1,128]{1,0:T(1,128)}, u32[]{:S(2)}) copy-start(f32[1,128]{1,0:T(1,128)} %get-tuple-element.32) | copy-start | bytes 1540
  114.7 47.9 %collective-permute-start = (bf16[128,1280]{1,0:T(8,128)(2,1)}, bf16[128,1280]{1,0:T(8,128)(2,1)}, u32[]{:S(2)}, u32[]{:S(2)}) collective-permute-start(bf16[128,1280]{1,0:T(8,128)(2,1)} %convert_element_type.63), channel_id=1, source_target_pairs={{0,1},{1,2},{2,3},{4,5},{5,6},{6,7},{8,9},{9,10},{10,11},{12,13},{... | collective-permute-start | bytes 983048 | tf_op jit(solution)/shard_map/ppermute | solution.py:405
  158.7 68.7 %all-to-all-start.2 = ((bf16[8,21,8,1280]{3,2,1,0:T(8,128)(2,1)}), bf16[8,21,8,1280]{3,2,1,0:T(8,128)(2,1)S(1)}, u32[]{:S(2)}, u32[]{:S(2)}) async-start(bf16[8,21,8,1280]{3,2,1,0:T(8,128)(2,1)} %collect.4), calls=%async_computation.2 | async-start | bytes 6881280 | tf_op jit(solution)/shard_map/all_to_all | solution.py:432
  162.5 18.7 %copy-start.3 = (bf16[256,5120]{1,0:T(8,128)(2,1)S(1)}, bf16[256,5120]{1,0:T(8,128)(2,1)}, u32[]{:S(2)}) copy-start(bf16[256,5120]{1,0:T(8,128)(2,1)} %copy-done.2) | copy-start | bytes 7864324
  164.0 11.0 %collective-permute-start.1 = (bf16[128,1280]{1,0:T(8,128)(2,1)S(1)}, bf16[128,1280]{1,0:T(8,128)(2,1)S(1)}, u32[]{:S(2)}, u32[]{:S(2)}) collective-permute-start(bf16[128,1280]{1,0:T(8,128)(2,1)S(1)} %add_convert_fusion.5), channel_id=1, source_target_pairs={{0,1},{1,2},{2,3},{4,5},{5,6},{6,7},{8,9},{9,10},{10,11},{12,13},{... | collective-permute-start | bytes 983048 | tf_op jit(solution)/shard_map/ppermute | solution.py:405
  176.2 11.0 %collective-permute-start.2 = (bf16[128,1280]{1,0:T(8,128)(2,1)S(1)}, bf16[128,1280]{1,0:T(8,128)(2,1)S(1)}, u32[]{:S(2)}, u32[]{:S(2)}) collective-permute-start(bf16[128,1280]{1,0:T(8,128)(2,1)S(1)} %add_convert_fusion.4), channel_id=1, source_target_pairs={{0,1},{1,2},{2,3},{4,5},{5,6},{6,7},{8,9},{9,10},{10,11},{12,13},{... | collective-permute-start | bytes 983048 | tf_op jit(solution)/shard_map/ppermute | solution.py:405
  187.3 0.7 copy-start.7
  222.1 25.9 %collective-permute-start.3 = (bf16[128,2560]{1,0:T(8,128)(2,1)}, bf16[128,2560]{1,0:T(8,128)(2,1)}, u32[]{:S(2)}, u32[]{:S(2)}) collective-permute-start(bf16[128,2560]{1,0:T(8,128)(2,1)} %convert_element_type.68), channel_id=1, source_target_pairs={{0,1},{1,2},{2,3},{4,5},{5,6},{6,7},{8,9},{9,10},{10,11},{12,13},{... | collective-permute-start | bytes 1966088 | tf_op jit(solution)/shard_map/ppermute | solution.py:405
  227.4 1.7 copy-start
  243.7 12.1 %copy-start.4 = (f32[128,1280]{1,0:T(8,128)S(1)}, f32[128,1280]{1,0:T(8,128)}, u32[]{:S(2)}) copy-start(f32[128,1280]{1,0:T(8,128)} %get-tuple-element.36) | copy-start | bytes 1966084
  244.9 24.9 %copy-start.1 = (f32[128,2560]{1,0:T(8,128)S(1)}, f32[128,2560]{1,0:T(8,128)}, u32[]{:S(2)}) copy-start(f32[128,2560]{1,0:T(8,128)} %get-tuple-element.35) | copy-start | bytes 3932164
  244.9 10.8 %collective-permute-start.6 = (bf16[128,1280]{1,0:T(8,128)(2,1)S(1)}, bf16[128,1280]{1,0:T(8,128)(2,1)S(1)}, u32[]{:S(2)}, u32[]{:S(2)}) collective-permute-start(bf16[128,1280]{1,0:T(8,128)(2,1)S(1)} %convert_element_type.73), channel_id=1, source_target_pairs={{0,1},{1,2},{2,3},{4,5},{5,6},{6,7},{8,9},{9,10},{10,11},{12,13},{... | collective-permute-start | bytes 983048 | tf_op jit(solution)/shard_map/ppermute | solution.py:405
  249.7 20.2 %collective-permute-start.4 = (bf16[128,2560]{1,0:T(8,128)(2,1)S(1)}, bf16[128,2560]{1,0:T(8,128)(2,1)S(1)}, u32[]{:S(2)}, u32[]{:S(2)}) collective-permute-start(bf16[128,2560]{1,0:T(8,128)(2,1)S(1)} %add_convert_fusion.1), channel_id=1, source_target_pairs={{0,1},{1,2},{2,3},{4,5},{5,6},{6,7},{8,9},{9,10},{10,11},{12,13},{... | collective-permute-start | bytes 1966088 | tf_op jit(solution)/shard_map/ppermute | solution.py:405
  255.9 21.0 %collective-permute-start.7 = (bf16[128,1280]{1,0:T(8,128)(2,1)S(1)}, bf16[128,1280]{1,0:T(8,128)(2,1)S(1)}, u32[]{:S(2)}, u32[]{:S(2)}) collective-permute-start(bf16[128,1280]{1,0:T(8,128)(2,1)S(1)} %add_convert_fusion.3), channel_id=1, source_target_pairs={{0,1},{1,2},{2,3},{4,5},{5,6},{6,7},{8,9},{9,10},{10,11},{12,13},{... | collective-permute-start | bytes 983048 | tf_op jit(solution)/shard_map/ppermute | solution.py:405
  270.0 20.9 %collective-permute-start.5 = (bf16[128,2560]{1,0:T(8,128)(2,1)S(1)}, bf16[128,2560]{1,0:T(8,128)(2,1)S(1)}, u32[]{:S(2)}, u32[]{:S(2)}) collective-permute-start(bf16[128,2560]{1,0:T(8,128)(2,1)S(1)} %add_convert_fusion), channel_id=1, source_target_pairs={{0,1},{1,2},{2,3},{4,5},{5,6},{6,7},{8,9},{9,10},{10,11},{12,13},{... | collective-permute-start | bytes 1966088 | tf_op jit(solution)/shard_map/ppermute | solution.py:405
  276.9 24.4 %collective-permute-start.8 = (bf16[128,1280]{1,0:T(8,128)(2,1)S(1)}, bf16[128,1280]{1,0:T(8,128)(2,1)S(1)}, u32[]{:S(2)}, u32[]{:S(2)}) collective-permute-start(bf16[128,1280]{1,0:T(8,128)(2,1)S(1)} %add_convert_fusion.2), channel_id=1, source_target_pairs={{0,1},{1,2},{2,3},{4,5},{5,6},{6,7},{8,9},{9,10},{10,11},{12,13},{... | collective-permute-start | bytes 983048 | tf_op jit(solution)/shard_map/ppermute | solution.py:405
  290.9 0.9 copy-start.5
  301.3 0.8 copy-start.6
